TPU v7x, 512 devices: a whole 4x8x8 slice. The times are simulated.
512 devices in a mesh: row: 32 (over x, y), col: 16 (over z, core).
Axes of the slice: x: 4, y: 8, z: 8, core: 2. Of those that a mesh axis runs over, the one named last changes fastest.
Arguments:
- features: bfloat16 [32, 2048, 256], P('row', 'col'), may hold values from -6 to 6
- weight: bfloat16 [256, 256], replicated, may hold values from -0.375 to 0.375
- tile_values: bfloat16 [32, 16, 48, 128, 128], P('row', 'col'), may hold values from -0.109375 to 0.109375
- tile_places: int32 [32, 16, 2, 48], P('row', 'col'), may hold values from 0 to 31, as said below
- tile_count: int32 [32, 16], P('row', 'col'), may hold values from 1 to 48, as said below
- upstream: bfloat16 [16, 4096, 256], P('col', 'row'), may hold values from -6 to 6
Outputs:
- activations: bfloat16 [16, 4096, 256], P('col', 'row')
- grad_features: bfloat16 [32, 2048, 256], P('row', 'col')
- grad_weight: float32 [256, 256], replicated
Inputs may be any that keep to these rules, and one draw needn't show every extreme that they name: `tile_places`: [r, c, 0, s] is a tile row, below 32, and [r, c, 1, s] a tile column, below 16, of slot s of block (r, c); positions may repeat, and repeated tiles add. `tile_count`: slots at or beyond this number hold no tile; some block is full.
All inputs are finite; a program needn't handle non-finite values.
Results may differ from a plain program's by a relative error of at most 0.02.
Values may be sent and summed in bfloat16 or wider, within the bound.
No kernel may reach another device: no remote copies, remote signals or barrier semaphores. Data moves between devices by JAX's collectives and lax.ppermute only.
A program may use at most 64 MiB of HBM per device.

v0:
```python
import math

import jax
import jax.numpy as jnp
from jax import lax
from jax.sharding import PartitionSpec as P


def silu_parts(pre_act):
    sigma = jax.nn.sigmoid(pre_act)
    return (pre_act * sigma, sigma * (1.0 + pre_act * (1.0 - sigma)))


def aggregate(tile_set, places, live_count, source, transpose, dest_tiles):
    tile_edge = tile_set.shape[-1]
    feat_width = source.shape[-1]
    slot_total = tile_set.shape[0]
    slot_group = math.gcd(slot_total, 8)
    source_tiles = source.reshape(source.shape[0] // tile_edge, tile_edge, feat_width)
    if transpose:
        take_all = places[0]
        put_all = places[1]
    else:
        take_all = places[1]
        put_all = places[0]

    def add_group(group_index, running):
        first_slot = group_index * slot_group
        tile_block = lax.dynamic_slice_in_dim(tile_set, first_slot, slot_group, 0)
        take_index = lax.dynamic_slice_in_dim(take_all, first_slot, slot_group, 0)
        put_index = lax.dynamic_slice_in_dim(put_all, first_slot, slot_group, 0)
        slab_rows = source_tiles[take_index]
        if transpose:
            products = jnp.einsum(
                "ski,skf->sif", tile_block, slab_rows, preferred_element_type=jnp.float32
            )
        else:
            products = jnp.einsum(
                "sik,skf->sif", tile_block, slab_rows, preferred_element_type=jnp.float32
            )
        live_mask = first_slot + jnp.arange(slot_group, dtype=jnp.int32) < live_count
        products = jnp.where(live_mask[:, None, None], products, jnp.float32(0.0))
        return running.at[put_index].add(products)

    zero_sum = jnp.zeros((dest_tiles, tile_edge, feat_width), jnp.float32)
    result = lax.fori_loop(0, slot_total // slot_group, add_group, zero_sum)
    return result.reshape(dest_tiles * tile_edge, feat_width)


def per_device(features, weight, tile_values, tile_places, tile_count, upstream):
    own_rows = features[0]
    up_rows = upstream[0]
    sub_rows = own_rows.shape[0]
    tile_set = tile_values[0, 0]
    places = tile_places[0, 0]
    live_count = tile_count[0, 0]
    tile_edge = tile_set.shape[-1]
    projected = jnp.dot(own_rows, weight, preferred_element_type=jnp.float32).astype(jnp.bfloat16)
    proj_panel = lax.all_gather(projected, "col", axis=0, tiled=True)
    forward_tiles = sub_rows * lax.axis_size("row") // tile_edge
    partial_value = aggregate(tile_set, places, live_count, proj_panel, False, forward_tiles)
    pre_act = lax.psum_scatter(
        partial_value.astype(jnp.bfloat16), "row", scatter_dimension=0, tiled=True
    ).astype(jnp.float32)
    out_rows, slope_part = silu_parts(pre_act)
    activations = out_rows.astype(jnp.bfloat16)
    slope_rows = (up_rows.astype(jnp.float32) * slope_part).astype(jnp.bfloat16)
    slope_panel = lax.all_gather(slope_rows, "row", axis=0, tiled=True)
    backward_tiles = sub_rows * lax.axis_size("col") // tile_edge
    back_partial = aggregate(tile_set, places, live_count, slope_panel, True, backward_tiles)
    grad_proj = lax.psum_scatter(
        back_partial.astype(jnp.bfloat16), "col", scatter_dimension=0, tiled=True
    )
    grad_features = lax.dot_general(
        grad_proj, weight, (((1,), (1,)), ((), ())), preferred_element_type=jnp.float32
    ).astype(jnp.bfloat16)
    weight_term = lax.dot_general(
        own_rows, grad_proj, (((0,), (0,)), ((), ())), preferred_element_type=jnp.float32
    )
    grad_weight = lax.psum(weight_term, ("row", "col"))
    return (activations[None], grad_features[None], grad_weight)


def solution(mesh):
    placed = (
        P("row", "col", None),
        P(),
        P("row", "col", None, None, None),
        P("row", "col", None, None),
        P("row", "col"),
        P("col", "row", None),
    )
    return jax.shard_map(
        per_device,
        mesh=mesh,
        in_specs=placed,
        out_specs=(P("col", "row", None), P("row", "col", None), P()),
        check_vma=False,
    )
```

profile of v0, /device:TPU:1, one launch (start us, length us, event | category | flops | bytes accessed | tf_op | source)
XLA Modules:
  0.0 793.0 jit_solution(10044786730707094419)
XLA Ops:
  8.1 1.6 convolution_convert_fusion.1
  10.5 47.9 %all-gather.3.cloned.1.call-done = bf16[2048,256]{1,0:T(8,128)(2,1)} async-done(((bf16[128,256]{1,0:T(8,128)(2,1)}), bf16[2048,256]{1,0:T(8,128)(2,1)}) %all-gather.3.cloned.1.call-update) | async-done | bytes 1048592 | tf_op jit(solution)/shard_map/all_gather | solution.py:59
  58.5 2.4 broadcast_in_dim.94
  60.9 35.3 %while.26 = (s32[]{:T(128)}, f32[32,128,256]{2,1,0:T(8,128)}, s32[48]{0:T(128)S(1)}, s32[]{:T(128)}, bf16[48,128,128]{2,1,0:T(8,128)(2,1)}, /*index=5*/s32[48]{0...) while((s32[]{:T(128)}, f32[32,128,256]{2,1,0:T(8,128)}, ...), condition=%wide.region_2.3_spmd, body=%wide.region_0.2_spmd.sunk | while | flops 67634248 | bytes 6033819 | solution.py:46
  63.5 3.4 scatter_fusion
  69.4 3.3 scatter_fusion
  75.3 3.3 scatter_fusion
  81.1 3.3 scatter_fusion
  87.0 3.3 scatter_fusion
  92.9 3.3 scatter_fusion
  96.2 3.8 convert_element_type.34
  100.1 216.6 %reduce-scatter.3.cloned.1.call-done = bf16[128,256]{1,0:T(8,128)(2,1)} async-done(((bf16[4096,256]{1,0:T(8,128)(2,1)}), bf16[128,256]{1,0:T(8,128)(2,1)}) %reduce-scatter.3.cloned.1.call-update) | async-done | bytes 65552 | tf_op jit(solution)/shard_map/reduce_scatter | solution.py:62
  319.3 83.5 %all-gather.5.cloned.1.call-done = bf16[4096,256]{1,0:T(8,128)(2,1)} async-done(((bf16[128,256]{1,0:T(8,128)(2,1)}), bf16[4096,256]{1,0:T(8,128)(2,1)}) %all-gather.5.cloned.1.call-update) | async-done | bytes 2097168 | tf_op jit(solution)/shard_map/all_gather | solution.py:68
  404.3 39.0 %while.27 = (s32[]{:T(128)}, f32[16,128,256]{2,1,0:T(8,128)}, s32[48]{0:T(128)S(1)}, s32[]{:T(128)}, bf16[48,128,128]{1,2,0:T(8,128)(2,1)S(1)}, /*index=5*/s32[4...) while((s32[]{:T(128)}, f32[16,128,256]{2,1,0:T(8,128)}, ...), condition=%wide.region_6.7_spmd, body=%wide.region_4.6_spmd.sunk | while | flops 67634248 | bytes 6034323 | solution.py:46
  404.4 2.2 gather_fusion.1
  407.5 3.3 scatter_fusion.1
  410.9 2.2 gather_fusion.1
  414.0 3.3 scatter_fusion.1
  417.4 2.2 gather_fusion.1
  420.6 3.3 scatter_fusion.1
  424.0 2.2 gather_fusion.1
  427.1 3.3 scatter_fusion.1
  430.5 2.2 gather_fusion.1
  433.6 3.2 scatter_fusion.1
  436.9 2.2 gather_fusion.1
  440.1 3.2 scatter_fusion.1
  443.3 2.7 convert_element_type.41
  446.1 61.3 %reduce-scatter.5.cloned.1.call-done = bf16[128,256]{1,0:T(8,128)(2,1)} async-done(((bf16[2048,256]{1,0:T(8,128)(2,1)}), bf16[128,256]{1,0:T(8,128)(2,1)}) %reduce-scatter.5.cloned.1.call-update) | async-done | bytes 65552 | tf_op jit(solution)/shard_map/reduce_scatter | solution.py:71
  507.4 1.8 convolution_bitcast_fusion
  509.2 1.7 fusion.4
  510.8 273.8 %all-reduce.2.cloned.1.call-done = f32[256,256]{0,1:T(8,128)} async-done(((f32[256,256]{0,1:T(8,128)}), f32[256,256]{0,1:T(8,128)}) %all-reduce.2.cloned.1.call-update) | async-done | bytes 262160 | tf_op jit(solution)/shard_map/psum | solution.py:80
  784.7 1.8 copy.11
  (78 shorter events, 27.3 us)
Async XLA Ops:
  7.2 0.9 copy-start
  7.2 51.3 %all-gather.3.cloned.1.call-start = ((), (), s32[]{:S(2)}) async-start(), calls=%async_computation.2 | async-start | bytes 1114112 | tf_op jit(solution)/shard_map/all_gather | solution.py:59
  9.7 307.0 %reduce-scatter.3.cloned.1.call-start = ((), (), s32[]{:S(2)}) async-start(), calls=%async_computation.3 | async-start | bytes 2162688 | tf_op jit(solution)/shard_map/reduce_scatter | solution.py:62
  58.5 2.4 copy-start.1
  100.0 216.7 %copy-start.4 = (bf16[1,128,256]{2,1,0:T(8,128)(2,1)S(1)}, bf16[1,128,256]{2,1,0:T(8,128)(2,1)}, u32[]{:S(2)}) copy-start(bf16[1,128,256]{2,1,0:T(8,128)(2,1)} %param.15) | copy-start | bytes 196612
  100.1 218.3 %copy-start.2 = (bf16[48,128,128]{2,1,0:T(8,128)(2,1)S(1)}, bf16[48,128,128]{2,1,0:T(8,128)(2,1)}, u32[]{:S(2)}) copy-start(bf16[48,128,128]{2,1,0:T(8,128)(2,1)} %get-tuple-element.467) | copy-start | bytes 4718596
  100.1 302.7 %all-gather.5.cloned.1.call-start = ((), (), s32[]{:S(2)}) async-start(), calls=%async_computation.4 | async-start | bytes 2162688 | tf_op jit(solution)/shard_map/all_gather | solution.py:68
  318.3 189.1 %reduce-scatter.5.cloned.1.call-start = ((), (), s32[]{:S(2)}) async-start(), calls=%async_computation.5 | async-start | bytes 1114112 | tf_op jit(solution)/shard_map/reduce_scatter | solution.py:71
  443.2 64.1 %copy-start.3 = (bf16[1,128,256]{2,1,0:T(8,128)(2,1)S(1)}, bf16[1,128,256]{2,1,0:T(8,128)(2,1)}, u32[]{:S(2)}) copy-start(bf16[1,128,256]{2,1,0:T(8,128)(2,1)} %param.10) | copy-start | bytes 196612
  446.0 338.7 %all-reduce.2.cloned.1.call-start = ((), (), s32[]{:S(2)}) async-start(), calls=%async_computation.6 | async-start | bytes 524288 | tf_op jit(solution)/shard_map/psum | solution.py:80
Sparse Core Ops, SparseCore 0:
  10.7 47.7 all-gather.2
  100.2 216.4 reduce-scatter.2
  320.5 82.2 all-gather.4
  446.1 61.2 reduce-scatter.4
  512.8 271.8 all-reduce.1
where the time goes:
time: 794 us; the launch traced here: 793 us
  waiting for transfers between devices  683 us (86%)
  other arithmetic  56.5 us (7%)
  local copies, waits for them, and re-layouts  24.8 us (3%)
  matrix products  14.2 us (2%)
  between operations  13.8 us (2%)
    psum x1, waiting for transfers between devices, per_device(): grad_weight = lax.psum(weight_term, ('row', 'col'))  274 us
    reduce_scatter x1, waiting for transfers between devices, per_device(): lax.psum_scatter(partial_value.astype(jnp.bfloat16), 'row', scatter_dimen...  217 us
    all_gather x1, waiting for transfers between devices, per_device(): slope_panel = lax.all_gather(slope_rows, 'row', axis=0, tiled=True)  83.5 us
    reduce_scatter x1, waiting for transfers between devices, per_device(): lax.psum_scatter(back_partial.astype(jnp.bfloat16), 'col', scatter_dimens...  61.3 us
    all_gather x1, waiting for transfers between devices, per_device(): proj_panel = lax.all_gather(projected, 'col', axis=0, tiled=True)  47.9 us
    scatter-add x12, other arithmetic, add_group(): return running.at[put_index].add(products)  39.6 us
    gather x12, local copies, waits for them, and re-layouts, add_group(): slab_rows = source_tiles[take_index]  16.5 us
  transfers between devices with their start and end apart: 5, of which 5 were waited for; matrix products, arithmetic and copies ran while one was open for 0% of the time, Pallas kernels for 0%

commit v1 on v0

v1 whole, which is shorter than its diff:
```python
import jax
import jax.numpy as jnp
from jax import lax
from jax.experimental import pallas as pl
from jax.experimental.pallas import tpu as pltpu
from jax.sharding import Mesh, PartitionSpec as P

BF = jnp.bfloat16
F32 = jnp.float32
VM = pl.BlockSpec(memory_space=pltpu.VMEM)
SM = pl.BlockSpec(memory_space=pltpu.SMEM)
T = 128
GROUP = 4


def call(kernel, outs, in_specs, *args, scratch=(), limit=24 << 20):
    return pl.pallas_call(
        kernel,
        out_shape=outs,
        in_specs=in_specs,
        out_specs=jax.tree.map(lambda _: VM, outs),
        scratch_shapes=scratch,
        compiler_params=pltpu.CompilerParams(vmem_limit_bytes=limit),
    )(*args)


def shape(dims, kind=BF):
    return jax.ShapeDtypeStruct(dims, kind)


def block_products(count_ref, tiles_ref, acc_ref, put, load, contract):
    slots = tiles_ref.shape[0]
    acc_ref[...] = jnp.zeros_like(acc_ref)
    count = count_ref[0, 0]

    def group(g, carry):
        products = []
        for k in range(GROUP):
            s = jnp.minimum(g * GROUP + k, slots - 1)
            product = lax.dot_general(
                tiles_ref[s], load(s), (((contract,), (0,)), ((), ())), preferred_element_type=F32
            )
            products.append((put(s), jnp.where(g * GROUP + k < count, product, 0.0)))
        for at, product in products:
            acc_ref[at] += product
        return carry

    lax.fori_loop(0, (count + GROUP - 1) // GROUP, group, 0)


def forward_kernel(places, count, tiles, own, other, out, acc):
    core = lax.axis_index("c")

    def load(s):
        col = places[1, s]
        z = col // 2
        return jnp.where(col % 2 == core, own[z], other[z])

    block_products(count, tiles, acc, lambda s: places[0, s], load, 1)
    out[...] = acc[...].astype(BF).reshape(out.shape)


def sum_kernel(parts, out):
    total = parts[0].astype(F32)
    for k in range(1, parts.shape[0]):
        total += parts[k].astype(F32)
    out[...] = total.astype(BF)


def node_kernel(parts, weight, upstream, act, send):
    agg = parts[0].astype(F32)
    for k in range(1, parts.shape[0]):
        agg += parts[k].astype(F32)
    agg = agg.astype(BF)
    pre = jnp.dot(agg, weight[...], preferred_element_type=F32)
    sigma = jax.nn.sigmoid(pre)
    act[...] = (pre * sigma).astype(BF)
    slope = (upstream[...].astype(F32) * sigma * (1.0 + pre * (1.0 - sigma))).astype(BF)
    back = lax.dot_general(
        slope, weight[...], (((1,), (1,)), ((), ())), preferred_element_type=F32
    ).astype(BF)
    term = lax.dot_general(agg, slope, (((0,), (0,)), ((), ())), preferred_element_type=F32)
    for y in range(8):
        send[y, :T] = back
        rows = [term[x * 64 + y * 8 : x * 64 + y * 8 + 8] for x in range(4)]
        send[y, T:] = jnp.concatenate(rows, 0).astype(BF)


def spread_kernel(got, send):
    term = got[0, T:].astype(F32)
    for k in range(1, 8):
        term += got[k, T:].astype(F32)
    high = term.astype(BF).astype(F32)
    low = term - high
    for x in range(4):
        for y in range(8):
            send[x, y * T : (y + 1) * T] = got[y, :T]
        rows = slice(x * 8, x * 8 + 8)
        send[x, 8 * T :] = jnp.concatenate([high[rows], low[rows]], 0).astype(BF)


def backward_kernel(places, count, tiles, got, keep, send, term, acc):
    core = lax.axis_index("c")

    def load(s):
        row = places[0, s]
        return got[row // 8, pl.ds(pl.multiple_of((row % 8) * T, T), T)]

    block_products(count, tiles, acc, lambda s: places[1, s], load, 0)
    for z in range(8):
        keep[z] = acc[2 * z + core].astype(BF)
        send[z * T : (z + 1) * T] = acc[2 * z + 1 - core].astype(BF)
    total = got[0, 8 * T :].astype(F32)
    for k in range(1, 4):
        total += got[k, 8 * T :].astype(F32)
    total = total[:8] + total[8:]
    term[...] = total
    high = total.astype(BF).astype(F32)
    send[8 * T :] = jnp.concatenate([high, total - high], 0).astype(BF)


def join_kernel(keep, got, term, send):
    other = got[8 * T :].astype(F32)
    total = term[...] + (other[:8] + other[8:])
    high = total.astype(BF).astype(F32)
    both = jnp.concatenate([high, total - high], 0).astype(BF)
    for z in range(8):
        send[z, :T] = (keep[z].astype(F32) + got[z * T : (z + 1) * T].astype(F32)).astype(BF)
        send[z, T:] = both


def last_kernel(got, grad, term):
    total = got[0].astype(F32)
    for k in range(1, 8):
        total += got[k].astype(F32)
    grad[...] = total[:T].astype(BF)
    rows = total[T : T + 8] + total[T + 8 :]
    for k in range(32):
        term[k] = rows


def per_device(features, weight, tile_values, tile_places, tile_count, upstream):
    own_rows = features[0]
    tiles = tile_values[0, 0]
    places = tile_places[0, 0]
    swap = [(0, 1), (1, 0)]

    own = lax.all_to_all(jnp.broadcast_to(own_rows, (8, T, 256)), "z", 0, 0)
    other = lax.ppermute(own, "c", swap)
    partial = call(
        forward_kernel, shape((4, 8 * T, 256)), [SM, SM, VM, VM, VM],
        places, tile_count, tiles, own, other, scratch=[pltpu.VMEM((32, T, 256), F32)],
    )
    parts = lax.all_to_all(partial, "x", 0, 0)
    parts = call(sum_kernel, shape((8 * T, 256)), [VM], parts)
    parts = lax.all_to_all(parts.reshape(8, T, 256), "y", 0, 0)
    act, send = call(
        node_kernel, (shape((T, 256)), shape((8, T + 32, 256))), [VM, VM, VM],
        parts, weight, upstream[0],
    )
    got = lax.all_to_all(send, "y", 0, 0)
    send = call(spread_kernel, shape((4, 8 * T + 16, 256)), [VM], got)
    got = lax.all_to_all(send, "x", 0, 0)
    keep, send, term = call(
        backward_kernel, (shape((8, T, 256)), shape((8 * T + 16, 256)), shape((8, 256), F32)),
        [SM, SM, VM, VM], places, tile_count, tiles, got,
        scratch=[pltpu.VMEM((16, T, 256), F32)],
    )
    got = lax.ppermute(send, "c", swap)
    send = call(join_kernel, shape((8, T + 16, 256)), [VM, VM, VM], keep, got, term)
    got = lax.all_to_all(send, "z", 0, 0)
    grad, term = call(last_kernel, (shape((T, 256)), shape((32, 8, 256), F32)), [VM], got)
    grad_weight = lax.all_to_all(term, ("x", "y"), 0, 0)
    return act[None], grad[None], grad_weight.reshape(256, 256)


def solution(mesh):
    fine = Mesh(mesh.devices.reshape(4, 8, 8, 2), ("x", "y", "z", "c"))
    row, col = ("x", "y"), ("z", "c")
    placed = (
        P(row, col, None),
        P(),
        P(row, col, None, None, None),
        P(row, col, None, None),
        P(row, col),
        P(col, row, None),
    )
    return jax.shard_map(
        per_device,
        mesh=fine,
        in_specs=placed,
        out_specs=(P(col, row, None), P(row, col, None), P()),
        check_vma=False,
    )
```

time: 794 us -> 189 us (0.24)
  waiting for transfers between devices: 683 us -> 2.39 us
  blocking collectives: 0 us -> 164 us
  other arithmetic: 56.5 us -> 0 us
  local copies, waits for them, and re-layouts: 24.8 us -> 2.39 us
  matrix products: 14.2 us -> 0 us
  between operations: 13.8 us -> 1.34 us
  starting transfers between devices: 0.21 us -> 10.3 us
    reduce_scatter x2 -> x0, waiting for transfers between devices: 278 us -> none  [the longest x1 217 us: per_device(): lax.psum_scatter(partial_value.astype(jnp.bfloat16), 'row', scatter_dimen...]
    psum x1 -> x0, waiting for transfers between devices: 274 us -> none  [per_device(): grad_weight = lax.psum(weight_term, ('row', 'col'))]
    all_to_all x0 -> x7, blocking collectives: none -> 164 us  [the longest x1 27.9 us: per_device(): parts = lax.all_to_all(parts.reshape(8, T, 256), 'y', 0, 0)]
    all_gather x2 -> x0, waiting for transfers between devices: 131 us -> none  [the longest x1 83.5 us: per_device(): slope_panel = lax.all_gather(slope_rows, 'row', axis=0, tiled=True)]
    scatter-add x12 -> x0, other arithmetic: 39.6 us -> none  [add_group(): return running.at[put_index].add(products)]
    gather x12 -> x0, local copies, waits for them, and re-layouts: 16.5 us -> none  [add_group(): slab_rows = source_tiles[take_index]]
    dot_general x15 -> x0, matrix products: 14.2 us -> none  [the longest x6 7.42 us: add_group(): jnp.einsum('sik,skf->sif', tile_block, slab_rows, preferred_element_type=...]
    ppermute x0 -> x2, starting transfers between devices: none -> 10.3 us  [the longest x1 6.04 us: per_device(): got = lax.ppermute(send, 'c', swap)]
  transfers between devices with their start and end apart: 5 -> 2, of which waited for: 5 -> 2; matrix products, arithmetic and copies ran while one was open for 0% -> 0% of each run, Pallas kernels for 0% -> 0%
where the time goes in v1:
time: 189 us; the launch traced here: 187 us
  blocking collectives  164 us (87%)
  starting transfers between devices  10.3 us (5%)
  Pallas kernels  5.93 us (3%)
  local copies, waits for them, and re-layouts  2.39 us (1%)
  waiting for transfers between devices  2.39 us (1%)
    all_to_all x1, blocking collectives, per_device(): parts = lax.all_to_all(parts.reshape(8, T, 256), 'y', 0, 0)  27.9 us
    all_to_all x1, blocking collectives, per_device(): parts = lax.all_to_all(partial, 'x', 0, 0)  26.9 us
    all_to_all x1, blocking collectives, per_device(): own = lax.all_to_all(jnp.broadcast_to(own_rows, (8, T, 256)), 'z', 0, 0)  26.8 us
    all_to_all x1, blocking collectives, per_device(): got = lax.all_to_all(send, 'x', 0, 0)  25.9 us
    all_to_all x1, blocking collectives, per_device(): got = lax.all_to_all(send, 'z', 0, 0)  23.2 us
    all_to_all x1, blocking collectives, per_device(): got = lax.all_to_all(send, 'y', 0, 0)  20.5 us
    all_to_all x1, blocking collectives, per_device(): grad_weight = lax.all_to_all(term, ('x', 'y'), 0, 0)  13.3 us
    ppermute x1, starting transfers between devices, per_device(): got = lax.ppermute(send, 'c', swap)  6.04 us
  transfers between devices with their start and end apart: 2, of which 2 were waited for; matrix products, arithmetic and copies ran while one was open for 0% of the time, Pallas kernels for 0%

profile of v1, /device:TPU:1, one launch (start us, length us, event | category | flops | bytes accessed | tf_op | source)
XLA Modules:
  0.0 186.7 jit_solution(14435613325865687775)
XLA Ops:
  0.6 0.0 copy-start
  0.6 1.0 broadcast_in_dim.9
  1.6 26.8 %all_to_all.35.own = bf16[8,128,256]{2,1,0:T(8,128)(2,1)S(1)} all-to-all(bf16[8,128,256]{2,1,0:T(8,128)(2,1)S(1)} %broadcast_in_dim.9), channel_id=1, replica_groups=mesh['x'=4,'y'=8,'z'=8,'c'=2] {'z'}, dimensions={0} | all-to-all | bytes 1048576 | tf_op jit(solution)/shard_map/all_to_all | solution.py:148
  28.4 4.2 %collective-permute-start = (bf16[8,128,256]{2,1,0:T(8,128)(2,1)S(1)}, bf16[8,128,256]{2,1,0:T(8,128)(2,1)S(1)}, u32[]{:S(2)}, u32[]{:S(2)}) collective-permute-start(bf16[8,128,256]{2,1,0:T(8,128)(2,1)S(1)} %all_to_all.35.own), channel_id=1, source_target_pairs={{0,1},{1,0},{2,3},{3,2},{4,5},{5,4},{6,7},{7,6},{8,9},{9,8},{10,11... | collective-permute-start | bytes 1572872 | tf_op jit(solution)/shard_map/ppermute | solution.py:149
  33.3 0.9 collective-permute-done.other
  34.2 0.0 copy-done
  34.2 0.0 copy-start.3
  34.2 0.7 copy-done.3
  34.8 2.0 %shard_map.85 = bf16[4,1024,256]{2,1,0:T(8,128)(2,1)S(1)} custom-call(s32[2,48]{1,0:T(2,128)S(1)} %bitcast.12, s32[1,1]{1,0:T(1,128)S(6)} %copy.10.count, bf16[48,128,128]{2,1,0:T(8,128)(2,1)S(1)} %bitcast.8, bf16[8,128,256]{2,1,0:T(8,128)(2,1)S(1)} %all_to_all.35.own, bf16[8,128,256]{2,1,0:T(8,128)(2,1)S(1)} %collective-permute-done.other), custom_call_target="tpu_custom_call" | custom-call | tf_op jit(solution)/shard_map/pallas_call | solution.py:17
  36.8 26.9 %all_to_all.36.parts = bf16[4,1024,256]{2,1,0:T(8,128)(2,1)S(1)} all-to-all(bf16[4,1024,256]{2,1,0:T(8,128)(2,1)S(1)} %shard_map.85), channel_id=1, replica_groups=mesh['x'=4,'y'=8,'z'=8,'c'=2] {'x'}, dimensions={0} | all-to-all | bytes 4194304 | tf_op jit(solution)/shard_map/all_to_all | solution.py:154
  63.7 0.0 copy-start.1
  63.7 0.0 copy-start.2
  63.7 0.3 shard_map.86
  64.0 27.9 %all_to_all.37.parts = bf16[8,128,256]{2,1,0:T(8,128)(2,1)S(1)} all-to-all(bf16[8,128,256]{2,1,0:T(8,128)(2,1)S(1)} %bitcast.10), channel_id=1, replica_groups=mesh['x'=4,'y'=8,'z'=8,'c'=2] {'y'}, dimensions={0} | all-to-all | bytes 1048576 | tf_op jit(solution)/shard_map/all_to_all | solution.py:156
  91.8 0.0 copy-done.1
  91.8 0.0 copy-done.2
  91.8 0.8 shard_map.87
  92.7 20.5 %all_to_all.38.got = bf16[8,160,256]{2,1,0:T(8,128)(2,1)S(1)} all-to-all(bf16[8,160,256]{2,1,0:T(8,128)(2,1)S(1)} %get-tuple-element.11), channel_id=1, replica_groups=mesh['x'=4,'y'=8,'z'=8,'c'=2] {'y'}, dimensions={0} | all-to-all | bytes 1310720 | tf_op jit(solution)/shard_map/all_to_all | solution.py:161
  113.1 0.1 shard_map.88
  113.3 0.0 copy-start.4
  113.3 25.9 %all_to_all.39.got = bf16[4,1040,256]{2,1,0:T(8,128)(2,1)S(1)} all-to-all(bf16[4,1040,256]{2,1,0:T(8,128)(2,1)S(1)} %shard_map.88), channel_id=1, replica_groups=mesh['x'=4,'y'=8,'z'=8,'c'=2] {'x'}, dimensions={0} | all-to-all | bytes 4259840 | tf_op jit(solution)/shard_map/all_to_all | solution.py:163
  139.2 0.0 copy-done.4
  139.2 1.9 shard_map.89
  141.1 6.0 %collective-permute-start.1 = (bf16[1040,256]{1,0:T(8,128)(2,1)S(1)}, bf16[1040,256]{1,0:T(8,128)(2,1)S(1)}, u32[]{:S(2)}, u32[]{:S(2)}) collective-permute-start(bf16[1040,256]{1,0:T(8,128)(2,1)S(1)} %get-tuple-element.13), channel_id=1, source_target_pairs={{0,1},{1,0},{2,3},{3,2},{4,5},{5,4},{6,7},{7,6},{8,9},{9,8},{10,11... | collective-permute-start | bytes 1597448 | tf_op jit(solution)/shard_map/ppermute | solution.py:169
  147.1 1.5 collective-permute-done.1.got
  148.7 0.1 shard_map.90
  148.8 23.2 %all_to_all.40.got = bf16[8,144,256]{2,1,0:T(8,128)(2,1)S(1)} all-to-all(bf16[8,144,256]{2,1,0:T(8,128)(2,1)S(1)} %shard_map.90), channel_id=1, replica_groups=mesh['x'=4,'y'=8,'z'=8,'c'=2] {'z'}, dimensions={0} | all-to-all | bytes 1179648 | tf_op jit(solution)/shard_map/all_to_all | solution.py:171
  172.0 0.7 shard_map.91
  172.7 13.3 %all_to_all.41 = f32[32,8,256]{2,1,0:T(8,128)S(1)} all-to-all(f32[32,8,256]{2,1,0:T(8,128)S(1)} %get-tuple-element.16), channel_id=1, replica_groups=mesh['x'=4,'y'=8,'z'=8,'c'=2] {'x','y'}, dimensions={0} | all-to-all | bytes 524288 | tf_op jit(solution)/shard_map/all_to_all | solution.py:173
  186.0 0.7 copy.11
Async XLA Ops:
  0.6 33.5 %copy-start = (bf16[1,1,48,128,128]{4,3,2,1,0:T(8,128)(2,1)S(1)}, bf16[1,1,48,128,128]{4,3,2,1,0:T(8,128)(2,1)}, u32[]{:S(2)}) copy-start(bf16[1,1,48,128,128]{4,3,2,1,0:T(8,128)(2,1)} %param.8) | copy-start | bytes 4718596
  28.4 5.8 %collective-permute-start = (bf16[8,128,256]{2,1,0:T(8,128)(2,1)S(1)}, bf16[8,128,256]{2,1,0:T(8,128)(2,1)S(1)}, u32[]{:S(2)}, u32[]{:S(2)}) collective-permute-start(bf16[8,128,256]{2,1,0:T(8,128)(2,1)S(1)} %all_to_all.35.own), channel_id=1, source_target_pairs={{0,1},{1,0},{2,3},{3,2},{4,5},{5,4},{6,7},{7,6},{8,9},{9,8},{10,11... | collective-permute-start | bytes 1572872 | tf_op jit(solution)/shard_map/ppermute | solution.py:149
  34.2 0.7 copy-start.3
  63.7 28.1 %copy-start.1 = (bf16[256,256]{1,0:T(8,128)(2,1)S(1)}, bf16[256,256]{1,0:T(8,128)(2,1)}, u32[]{:S(2)}) copy-start(bf16[256,256]{1,0:T(8,128)(2,1)} %weight.1) | copy-start | bytes 393220
  63.7 28.1 %copy-start.2 = (bf16[1,128,256]{2,1,0:T(8,128)(2,1)S(1)}, bf16[1,128,256]{2,1,0:T(8,128)(2,1)}, u32[]{:S(2)}) copy-start(bf16[1,128,256]{2,1,0:T(8,128)(2,1)} %param.11) | copy-start | bytes 196612
  113.3 26.0 %copy-start.4 = (s32[1,1,2,48]{3,2,1,0:T(2,128)S(1)}, s32[1,1,2,48]{3,2,1,0:T(2,128)}, u32[]{:S(2)}) copy-start(s32[1,1,2,48]{3,2,1,0:T(2,128)} %param.9) | copy-start | bytes 1156
  141.1 7.6 %collective-permute-start.1 = (bf16[1040,256]{1,0:T(8,128)(2,1)S(1)}, bf16[1040,256]{1,0:T(8,128)(2,1)S(1)}, u32[]{:S(2)}, u32[]{:S(2)}) collective-permute-start(bf16[1040,256]{1,0:T(8,128)(2,1)S(1)} %get-tuple-element.13), channel_id=1, source_target_pairs={{0,1},{1,0},{2,3},{3,2},{4,5},{5,4},{6,7},{7,6},{8,9},{9,8},{10,11... | collective-permute-start | bytes 1597448 | tf_op jit(solution)/shard_map/ppermute | solution.py:169

commit v2 on v1

--- a/solution.py
+++ b/solution.py
@@ -82,24 +82,20 @@
     term = lax.dot_general(agg, slope, (((0,), (0,)), ((), ())), preferred_element_type=F32)
     for y in range(8):
         send[y, :T] = back
-        rows = [term[x * 64 + y * 8 : x * 64 + y * 8 + 8] for x in range(4)]
-        send[y, T:] = jnp.concatenate(rows, 0).astype(BF)
+        send[y, T:] = term[y * 32 : y * 32 + 32].astype(BF)
 
 
-def spread_kernel(got, send):
-    term = got[0, T:].astype(F32)
+def spread_kernel(got, send, term):
+    total = got[0, T:].astype(F32)
     for k in range(1, 8):
-        term += got[k, T:].astype(F32)
-    high = term.astype(BF).astype(F32)
-    low = term - high
+        total += got[k, T:].astype(F32)
+    term[...] = total
     for x in range(4):
         for y in range(8):
             send[x, y * T : (y + 1) * T] = got[y, :T]
-        rows = slice(x * 8, x * 8 + 8)
-        send[x, 8 * T :] = jnp.concatenate([high[rows], low[rows]], 0).astype(BF)
 
 
-def backward_kernel(places, count, tiles, got, keep, send, term, acc):
+def backward_kernel(places, count, tiles, got, keep, send, acc):
     core = lax.axis_index("c")
 
     def load(s):
@@ -109,34 +105,25 @@
     block_products(count, tiles, acc, lambda s: places[1, s], load, 0)
     for z in range(8):
         keep[z] = acc[2 * z + core].astype(BF)
-        send[z * T : (z + 1) * T] = acc[2 * z + 1 - core].astype(BF)
-    total = got[0, 8 * T :].astype(F32)
-    for k in range(1, 4):
-        total += got[k, 8 * T :].astype(F32)
-    total = total[:8] + total[8:]
-    term[...] = total
-    high = total.astype(BF).astype(F32)
-    send[8 * T :] = jnp.concatenate([high, total - high], 0).astype(BF)
+        send[z] = acc[2 * z + 1 - core].astype(BF)
 
 
-def join_kernel(keep, got, term, send):
-    other = got[8 * T :].astype(F32)
-    total = term[...] + (other[:8] + other[8:])
-    high = total.astype(BF).astype(F32)
-    both = jnp.concatenate([high, total - high], 0).astype(BF)
-    for z in range(8):
-        send[z, :T] = (keep[z].astype(F32) + got[z * T : (z + 1) * T].astype(F32)).astype(BF)
-        send[z, T:] = both
+def join_kernel(keep, got, send):
+    send[...] = (keep[...].astype(F32) + got[...].astype(F32)).astype(BF)
 
 
-def last_kernel(got, grad, term):
-    total = got[0].astype(F32)
-    for k in range(1, 8):
-        total += got[k].astype(F32)
-    grad[...] = total[:T].astype(BF)
-    rows = total[T : T + 8] + total[T + 8 :]
-    for k in range(32):
-        term[k] = rows
+def gather_kernel(pair, quad, rest, out):
+    y = lax.axis_index("y")
+    for k in range(2):
+        out[y ^ k] = pair[k * 32 : k * 32 + 32]
+        out[y ^ (k + 2)] = quad[k * 32 : k * 32 + 32]
+    for k in range(4):
+        out[y ^ (k + 4)] = rest[k * 32 : k * 32 + 32]
+
+
+def swap_with(value, axis, bits):
+    size = lax.axis_size(axis)
+    return lax.ppermute(value, axis, [(i, i ^ bits) for i in range(size)])
 
 
 def per_device(features, weight, tile_values, tile_places, tile_count, upstream):
@@ -159,18 +146,24 @@
         parts, weight, upstream[0],
     )
     got = lax.all_to_all(send, "y", 0, 0)
-    send = call(spread_kernel, shape((4, 8 * T + 16, 256)), [VM], got)
+    send, term = call(
+        spread_kernel, (shape((4, 8 * T, 256)), shape((32, 256), F32)), [VM], got
+    )
     got = lax.all_to_all(send, "x", 0, 0)
-    keep, send, term = call(
-        backward_kernel, (shape((8, T, 256)), shape((8 * T + 16, 256)), shape((8, 256), F32)),
-        [SM, SM, VM, VM], places, tile_count, tiles, got,
-        scratch=[pltpu.VMEM((16, T, 256), F32)],
+    for axis, bits in (("x", 1), ("x", 3), ("c", 1), ("z", 1), ("z", 2), ("z", 4)):
+        term = term + swap_with(term, axis, bits)
+    keep, send = call(
+        backward_kernel, (shape((8, T, 256)), shape((8, T, 256))), [SM, SM, VM, VM],
+        places, tile_count, tiles, got, scratch=[pltpu.VMEM((16, T, 256), F32)],
     )
     got = lax.ppermute(send, "c", swap)
-    send = call(join_kernel, shape((8, T + 16, 256)), [VM, VM, VM], keep, got, term)
+    send = call(join_kernel, shape((8, T, 256)), [VM, VM], keep, got)
     got = lax.all_to_all(send, "z", 0, 0)
-    grad, term = call(last_kernel, (shape((T, 256)), shape((32, 8, 256), F32)), [VM], got)
-    grad_weight = lax.all_to_all(term, ("x", "y"), 0, 0)
+    pair = jnp.concatenate([term, swap_with(term, "y", 1)], 0)
+    quad = swap_with(pair, "y", 2)
+    rest = swap_with(jnp.concatenate([pair, quad], 0), "y", 4)
+    grad_weight = call(gather_kernel, shape((8, 32, 256), F32), [VM, VM, VM], pair, quad, rest)
+    grad = call(sum_kernel, shape((T, 256)), [VM], got)
     return act[None], grad[None], grad_weight.reshape(256, 256)
 
 

time: 189 us -> 219 us (1.16)
  the two profiles are of different devices: /device:TPU:1 before, /device:TPU:64 now
where the time goes in v2:
time: 219 us; the launch traced here: 218 us
  blocking collectives  128 us (58%)
  waiting for transfers between devices  40.3 us (18%)
  starting transfers between devices  38.3 us (17%)
  Pallas kernels  8.44 us (4%)
    ppermute x9, waiting for transfers between devices, swap_with(): return lax.ppermute(value, axis, [(i, i ^ bits) for i in range(size)])  37.2 us
    all_to_all x1, blocking collectives, per_device(): parts = lax.all_to_all(partial, 'x', 0, 0)  31.6 us
    ppermute x9, starting transfers between devices, swap_with(): return lax.ppermute(value, axis, [(i, i ^ bits) for i in range(size)])  27.6 us
    all_to_all x1, blocking collectives, per_device(): got = lax.all_to_all(send, 'x', 0, 0)  26 us
    all_to_all x1, blocking collectives, per_device(): own = lax.all_to_all(jnp.broadcast_to(own_rows, (8, T, 256)), 'z', 0, 0)  25.8 us
    all_to_all x1, blocking collectives, per_device(): parts = lax.all_to_all(parts.reshape(8, T, 256), 'y', 0, 0)  23.6 us
    all_to_all x1, blocking collectives, per_device(): got = lax.all_to_all(send, 'y', 0, 0)  21.1 us
    pallas_call x8, Pallas kernels, call(): pl.pallas_call(kernel, out_shape=outs, in_specs=in_specs, out_specs=jax.t...  8.44 us
  transfers between devices with their start and end apart: 12, of which 11 were waited for; matrix products, arithmetic and copies ran while one was open for 0% of the time, Pallas kernels for 0%

profile of v2, /device:TPU:64, one launch (start us, length us, event | category | flops | bytes accessed | tf_op | source)
XLA Modules:
  0.0 218.4 jit_solution(16054113113576456372)
XLA Ops:
  0.6 1.0 broadcast_in_dim.9
  1.6 25.8 %all_to_all.30.own = bf16[8,128,256]{2,1,0:T(8,128)(2,1)S(1)} all-to-all(bf16[8,128,256]{2,1,0:T(8,128)(2,1)S(1)} %broadcast_in_dim.9), channel_id=1, replica_groups=mesh['x'=4,'y'=8,'z'=8,'c'=2] {'z'}, dimensions={0} | all-to-all | bytes 1048576 | tf_op jit(solution)/shard_map/all_to_all | solution.py:135
  27.4 1.9 collective-permute-start
  30.0 1.2 collective-permute-done.other
  31.9 2.5 %shard_map.85 = bf16[4,1024,256]{2,1,0:T(8,128)(2,1)S(1)} custom-call(s32[2,48]{1,0:T(2,128)S(1)} %bitcast.12, s32[1,1]{1,0:T(1,128)S(6)} %copy.9.count, bf16[48,128,128]{2,1,0:T(8,128)(2,1)S(1)} %bitcast.8, bf16[8,128,256]{2,1,0:T(8,128)(2,1)S(1)} %all_to_all.30.own, bf16[8,128,256]{2,1,0:T(8,128)(2,1)S(1)} %collective-permute-done.other), custom_call_target="tpu_custom_call" | custom-call | tf_op jit(solution)/shard_map/pallas_call | solution.py:17
  34.4 31.6 %all_to_all.31.parts = bf16[4,1024,256]{2,1,0:T(8,128)(2,1)S(1)} all-to-all(bf16[4,1024,256]{2,1,0:T(8,128)(2,1)S(1)} %shard_map.85), channel_id=1, replica_groups=mesh['x'=4,'y'=8,'z'=8,'c'=2] {'x'}, dimensions={0} | all-to-all | bytes 4194304 | tf_op jit(solution)/shard_map/all_to_all | solution.py:141
  66.3 23.6 %all_to_all.32.parts = bf16[8,128,256]{2,1,0:T(8,128)(2,1)S(1)} all-to-all(bf16[8,128,256]{2,1,0:T(8,128)(2,1)S(1)} %bitcast.10), channel_id=1, replica_groups=mesh['x'=4,'y'=8,'z'=8,'c'=2] {'y'}, dimensions={0} | all-to-all | bytes 1048576 | tf_op jit(solution)/shard_map/all_to_all | solution.py:143
  90.7 21.1 %all_to_all.33.got = bf16[8,160,256]{2,1,0:T(8,128)(2,1)S(1)} all-to-all(bf16[8,160,256]{2,1,0:T(8,128)(2,1)S(1)} %get-tuple-element.10), channel_id=1, replica_groups=mesh['x'=4,'y'=8,'z'=8,'c'=2] {'y'}, dimensions={0} | all-to-all | bytes 1310720 | tf_op jit(solution)/shard_map/all_to_all | solution.py:148
  112.0 26.0 %all_to_all.34.got = bf16[4,1024,256]{2,1,0:T(8,128)(2,1)S(1)} all-to-all(bf16[4,1024,256]{2,1,0:T(8,128)(2,1)S(1)} %get-tuple-element.11), channel_id=1, replica_groups=mesh['x'=4,'y'=8,'z'=8,'c'=2] {'x'}, dimensions={0} | all-to-all | bytes 4194304 | tf_op jit(solution)/shard_map/all_to_all | solution.py:152
  138.0 2.4 %shard_map.89 = (bf16[8,128,256]{2,1,0:T(8,128)(2,1)S(1)}, bf16[8,128,256]{2,1,0:T(8,128)(2,1)S(1)}) custom-call(s32[2,48]{1,0:T(2,128)S(1)} %bitcast.13, s32[1,1]{1,0:T(1,128)S(6)} %copy.9.count, bf16[48,128,128]{2,1,0:T(8,128)(2,1)S(1)} %bitcast.9, bf16[4,1024,256]{2,1,0:T(8,128)(2,1)S(1)} %all_to_all.34.got), custom_call_target="tpu_custom_call" | custom-call | tf_op jit(solution)/shard_map/pallas_call | solution.py:17
  140.4 1.9 collective-permute-start.1
  142.3 1.9 collective-permute-done.1.got
  144.2 0.9 shard_map.90
  145.1 6.9 %all-to-all-start.5 = ((bf16[8,128,256]{2,1,0:T(8,128)(2,1)}), bf16[8,128,256]{2,1,0:T(8,128)(2,1)S(1)}, u32[]{:S(2)}, u32[]{:S(2)}) async-start(bf16[8,128,256]{2,1,0:T(8,128)(2,1)} %shard_map.90), calls=%async_computation.5 | async-start | bytes 1048576 | tf_op jit(solution)/shard_map/all_to_all | solution.py:161
  152.0 5.1 %collective-permute-start.2 = (f32[32,256]{1,0:T(8,128)S(1)}, f32[32,256]{1,0:T(8,128)S(1)}, u32[]{:S(2)}, u32[]{:S(2)}) collective-permute-start(f32[32,256]{1,0:T(8,128)S(1)} %get-tuple-element.14), channel_id=1, source_target_pairs={{0,128},{128,0},{256,384},{384,256},{1,129},{129,1},{257,385},{385... | collective-permute-start | bytes 98312 | tf_op jit(solution)/shard_map/ppermute | solution.py:126
  157.1 1.9 collective-permute-done.2
  159.0 1.9 collective-permute-start.3
  160.9 5.1 %collective-permute-done.3 = f32[32,256]{1,0:T(8,128)S(1)} collective-permute-done((f32[32,256]{1,0:T(8,128)S(1)}, f32[32,256]{1,0:T(8,128)S(1)}, u32[]{:S(2)}, u32[]{:S(2)}) %collective-permute-start.3) | collective-permute-done | bytes 32800 | tf_op jit(solution)/shard_map/ppermute | solution.py:126
  166.0 1.9 collective-permute-start.4
  167.9 1.2 collective-permute-done.4
  169.1 1.9 collective-permute-start.5
  171.0 3.9 %collective-permute-done.5 = f32[32,256]{1,0:T(8,128)S(1)} collective-permute-done((f32[32,256]{1,0:T(8,128)S(1)}, f32[32,256]{1,0:T(8,128)S(1)}, u32[]{:S(2)}, u32[]{:S(2)}) %collective-permute-start.5) | collective-permute-done | bytes 32800 | tf_op jit(solution)/shard_map/ppermute | solution.py:126
  174.9 4.3 %collective-permute-start.6 = (f32[32,256]{1,0:T(8,128)S(1)}, f32[32,256]{1,0:T(8,128)S(1)}, u32[]{:S(2)}, u32[]{:S(2)}) collective-permute-start(f32[32,256]{1,0:T(8,128)S(1)} %add.21), channel_id=1, source_target_pairs={{0,4},{2,6},{4,0},{6,2},{8,12},{10,14},{12,8},{14,10},{1,5},{3,7},... | collective-permute-start | bytes 98312 | tf_op jit(solution)/shard_map/ppermute | solution.py:126
  179.2 2.4 %collective-permute-done.6 = f32[32,256]{1,0:T(8,128)S(1)} collective-permute-done((f32[32,256]{1,0:T(8,128)S(1)}, f32[32,256]{1,0:T(8,128)S(1)}, u32[]{:S(2)}, u32[]{:S(2)}) %collective-permute-start.6) | collective-permute-done | bytes 32800 | tf_op jit(solution)/shard_map/ppermute | solution.py:126
  181.6 6.5 %collective-permute-start.7 = (f32[32,256]{1,0:T(8,128)S(1)}, f32[32,256]{1,0:T(8,128)S(1)}, u32[]{:S(2)}, u32[]{:S(2)}) collective-permute-start(f32[32,256]{1,0:T(8,128)S(1)} %add.22), channel_id=1, source_target_pairs={{0,8},{2,10},{4,12},{6,14},{8,0},{10,2},{12,4},{14,6},{1,9},{3,11}... | collective-permute-start | bytes 98312 | tf_op jit(solution)/shard_map/ppermute | solution.py:126
  188.1 3.2 %collective-permute-done.7 = f32[32,256]{1,0:T(8,128)S(1)} collective-permute-done((f32[32,256]{1,0:T(8,128)S(1)}, f32[32,256]{1,0:T(8,128)S(1)}, u32[]{:S(2)}, u32[]{:S(2)}) %collective-permute-start.7) | collective-permute-done | bytes 32800 | tf_op jit(solution)/shard_map/ppermute | solution.py:126
  191.3 2.2 collective-permute-start.8
  193.5 3.6 %collective-permute-done.8 = f32[32,256]{1,0:T(8,128)S(1)} collective-permute-done((f32[32,256]{1,0:T(8,128)S(1)}, f32[32,256]{1,0:T(8,128)S(1)}, u32[]{:S(2)}, u32[]{:S(2)}) %collective-permute-start.8) | collective-permute-done | bytes 32800 | tf_op jit(solution)/shard_map/ppermute | solution.py:126
  197.1 1.9 collective-permute-start.9
  199.1 6.9 %collective-permute-done.9.quad = f32[64,256]{1,0:T(8,128)S(1)} collective-permute-done((f32[64,256]{1,0:T(8,128)S(1)}, f32[64,256]{1,0:T(8,128)S(1)}, u32[]{:S(2)}, u32[]{:S(2)}) %collective-permute-start.9) | collective-permute-done | bytes 65568 | tf_op jit(solution)/shard_map/ppermute | solution.py:126
  206.0 1.9 collective-permute-start.10
  207.9 9.0 %collective-permute-done.10.rest = f32[128,256]{1,0:T(8,128)S(1)} collective-permute-done((f32[128,256]{1,0:T(8,128)S(1)}, f32[128,256]{1,0:T(8,128)S(1)}, u32[]{:S(2)}, u32[]{:S(2)}) %collective-permute-start.10) | collective-permute-done | bytes 131104 | tf_op jit(solution)/shard_map/ppermute | solution.py:126
  (24 shorter events, 3.4 us)
Async XLA Ops:
  0.6 30.6 %copy-start = (bf16[1,1,48,128,128]{4,3,2,1,0:T(8,128)(2,1)S(1)}, bf16[1,1,48,128,128]{4,3,2,1,0:T(8,128)(2,1)}, u32[]{:S(2)}) copy-start(bf16[1,1,48,128,128]{4,3,2,1,0:T(8,128)(2,1)} %param.8) | copy-start | bytes 4718596
  27.4 3.8 %collective-permute-start = (bf16[8,128,256]{2,1,0:T(8,128)(2,1)S(1)}, bf16[8,128,256]{2,1,0:T(8,128)(2,1)S(1)}, u32[]{:S(2)}, u32[]{:S(2)}) collective-permute-start(bf16[8,128,256]{2,1,0:T(8,128)(2,1)S(1)} %all_to_all.30.own), channel_id=1, source_target_pairs={{0,1},{1,0},{2,3},{3,2},{4,5},{5,4},{6,7},{7,6},{8,9},{9,8},{10,11... | collective-permute-start | bytes 1572872 | tf_op jit(solution)/shard_map/ppermute | solution.py:136
  31.2 0.7 copy-start.3
  66.0 23.9 %copy-start.1 = (bf16[256,256]{1,0:T(8,128)(2,1)S(1)}, bf16[256,256]{1,0:T(8,128)(2,1)}, u32[]{:S(2)}) copy-start(bf16[256,256]{1,0:T(8,128)(2,1)} %weight.1) | copy-start | bytes 393220
  66.0 23.9 %copy-start.2 = (bf16[1,128,256]{2,1,0:T(8,128)(2,1)S(1)}, bf16[1,128,256]{2,1,0:T(8,128)(2,1)}, u32[]{:S(2)}) copy-start(bf16[1,128,256]{2,1,0:T(8,128)(2,1)} %param.11) | copy-start | bytes 196612
  112.0 26.0 %copy-start.4 = (s32[1,1,2,48]{3,2,1,0:T(2,128)S(1)}, s32[1,1,2,48]{3,2,1,0:T(2,128)}, u32[]{:S(2)}) copy-start(s32[1,1,2,48]{3,2,1,0:T(2,128)} %param.9) | copy-start | bytes 1156
  140.4 3.8 %collective-permute-start.1 = (bf16[8,128,256]{2,1,0:T(8,128)(2,1)S(1)}, bf16[8,128,256]{2,1,0:T(8,128)(2,1)S(1)}, u32[]{:S(2)}, u32[]{:S(2)}) collective-permute-start(bf16[8,128,256]{2,1,0:T(8,128)(2,1)S(1)} %get-tuple-element.13), channel_id=1, source_target_pairs={{0,1},{1,0},{2,3},{3,2},{4,5},{5,4},{6,7},{7,6},{8,9},{9,8},{10,11... | collective-permute-start | bytes 1572872 | tf_op jit(solution)/shard_map/ppermute | solution.py:159
  145.1 72.5 %all-to-all-start.5 = ((bf16[8,128,256]{2,1,0:T(8,128)(2,1)}), bf16[8,128,256]{2,1,0:T(8,128)(2,1)S(1)}, u32[]{:S(2)}, u32[]{:S(2)}) async-start(bf16[8,128,256]{2,1,0:T(8,128)(2,1)} %shard_map.90), calls=%async_computation.5 | async-start | bytes 1048576 | tf_op jit(solution)/shard_map/all_to_all | solution.py:161
  152.0 7.0 %collective-permute-start.2 = (f32[32,256]{1,0:T(8,128)S(1)}, f32[32,256]{1,0:T(8,128)S(1)}, u32[]{:S(2)}, u32[]{:S(2)}) collective-permute-start(f32[32,256]{1,0:T(8,128)S(1)} %get-tuple-element.14), channel_id=1, source_target_pairs={{0,128},{128,0},{256,384},{384,256},{1,129},{129,1},{257,385},{385... | collective-permute-start | bytes 98312 | tf_op jit(solution)/shard_map/ppermute | solution.py:126
  159.0 7.0 %collective-permute-start.3 = (f32[32,256]{1,0:T(8,128)S(1)}, f32[32,256]{1,0:T(8,128)S(1)}, u32[]{:S(2)}, u32[]{:S(2)}) collective-permute-start(f32[32,256]{1,0:T(8,128)S(1)} %add.18), channel_id=1, source_target_pairs={{0,384},{128,256},{256,128},{384,0},{1,385},{129,257},{257,129},{3... | collective-permute-start | bytes 98312 | tf_op jit(solution)/shard_map/ppermute | solution.py:126
  166.0 3.1 %collective-permute-start.4 = (f32[32,256]{1,0:T(8,128)S(1)}, f32[32,256]{1,0:T(8,128)S(1)}, u32[]{:S(2)}, u32[]{:S(2)}) collective-permute-start(f32[32,256]{1,0:T(8,128)S(1)} %add.19), channel_id=1, source_target_pairs={{0,1},{1,0},{2,3},{3,2},{4,5},{5,4},{6,7},{7,6},{8,9},{9,8},{10,11... | collective-permute-start | bytes 98312 | tf_op jit(solution)/shard_map/ppermute | solution.py:126
  169.1 5.8 %collective-permute-start.5 = (f32[32,256]{1,0:T(8,128)S(1)}, f32[32,256]{1,0:T(8,128)S(1)}, u32[]{:S(2)}, u32[]{:S(2)}) collective-permute-start(f32[32,256]{1,0:T(8,128)S(1)} %add.20), channel_id=1, source_target_pairs={{0,2},{2,0},{4,6},{6,4},{8,10},{10,8},{12,14},{14,12},{1,3},{3,1},... | collective-permute-start | bytes 98312 | tf_op jit(solution)/shard_map/ppermute | solution.py:126
  174.9 6.7 %collective-permute-start.6 = (f32[32,256]{1,0:T(8,128)S(1)}, f32[32,256]{1,0:T(8,128)S(1)}, u32[]{:S(2)}, u32[]{:S(2)}) collective-permute-start(f32[32,256]{1,0:T(8,128)S(1)} %add.21), channel_id=1, source_target_pairs={{0,4},{2,6},{4,0},{6,2},{8,12},{10,14},{12,8},{14,10},{1,5},{3,7},... | collective-permute-start | bytes 98312 | tf_op jit(solution)/shard_map/ppermute | solution.py:126
  181.6 9.7 %collective-permute-start.7 = (f32[32,256]{1,0:T(8,128)S(1)}, f32[32,256]{1,0:T(8,128)S(1)}, u32[]{:S(2)}, u32[]{:S(2)}) collective-permute-start(f32[32,256]{1,0:T(8,128)S(1)} %add.22), channel_id=1, source_target_pairs={{0,8},{2,10},{4,12},{6,14},{8,0},{10,2},{12,4},{14,6},{1,9},{3,11}... | collective-permute-start | bytes 98312 | tf_op jit(solution)/shard_map/ppermute | solution.py:126
  191.3 5.8 %collective-permute-start.8 = (f32[32,256]{1,0:T(8,128)S(1)}, f32[32,256]{1,0:T(8,128)S(1)}, u32[]{:S(2)}, u32[]{:S(2)}) collective-permute-start(f32[32,256]{1,0:T(8,128)S(1)} %add.23), channel_id=1, source_target_pairs={{0,16},{16,0},{32,48},{48,32},{64,80},{80,64},{96,112},{112,96},{1... | collective-permute-start | bytes 98312 | tf_op jit(solution)/shard_map/ppermute | solution.py:126
  197.1 8.9 %collective-permute-start.9 = (f32[64,256]{1,0:T(8,128)S(1)}, f32[64,256]{1,0:T(8,128)S(1)}, u32[]{:S(2)}, u32[]{:S(2)}) collective-permute-start(f32[64,256]{1,0:T(8,128)S(1)} %pad_maximum_fusion.1.pair), channel_id=1, source_target_pairs={{0,32},{16,48},{32,0},{48,16},{64,96},{80,112},{96,64},{112,80},{1... | collective-permute-start | bytes 196616 | tf_op jit(solution)/shard_map/ppermute | solution.py:126
  206.0 10.9 %collective-permute-start.10 = (f32[128,256]{1,0:T(8,128)S(1)}, f32[128,256]{1,0:T(8,128)S(1)}, u32[]{:S(2)}, u32[]{:S(2)}) collective-permute-start(f32[128,256]{1,0:T(8,128)S(1)} %pad_maximum_fusion), channel_id=1, source_target_pairs={{0,64},{16,80},{32,96},{48,112},{64,0},{80,16},{96,32},{112,48},{1... | collective-permute-start | bytes 393224 | tf_op jit(solution)/shard_map/ppermute | solution.py:126

commit v3 on v1

--- a/solution.py
+++ b/solution.py
@@ -57,7 +57,9 @@
         return jnp.where(col % 2 == core, own[z], other[z])
 
     block_products(count, tiles, acc, lambda s: places[0, s], load, 1)
-    out[...] = acc[...].astype(BF).reshape(out.shape)
+    for row in range(32):
+        at = (row % 8) // 2 * T
+        out[row // 8 * 2 + row % 2, at : at + T] = acc[row].astype(BF)
 
 
 def sum_kernel(parts, out):
@@ -80,23 +82,24 @@
         slope, weight[...], (((1,), (1,)), ((), ())), preferred_element_type=F32
     ).astype(BF)
     term = lax.dot_general(agg, slope, (((0,), (0,)), ((), ())), preferred_element_type=F32)
-    for y in range(8):
-        send[y, :T] = back
-        rows = [term[x * 64 + y * 8 : x * 64 + y * 8 + 8] for x in range(4)]
-        send[y, T:] = jnp.concatenate(rows, 0).astype(BF)
+    for h in range(4):
+        send[h, :T] = back
+        for x in range(4):
+            at = x * 64 + h * 16
+            send[h, T + x * 16 : T + x * 16 + 16] = term[at : at + 16].astype(BF)
 
 
 def spread_kernel(got, send):
     term = got[0, T:].astype(F32)
-    for k in range(1, 8):
+    for k in range(1, 4):
         term += got[k, T:].astype(F32)
     high = term.astype(BF).astype(F32)
     low = term - high
-    for x in range(4):
-        for y in range(8):
-            send[x, y * T : (y + 1) * T] = got[y, :T]
-        rows = slice(x * 8, x * 8 + 8)
-        send[x, 8 * T :] = jnp.concatenate([high[rows], low[rows]], 0).astype(BF)
+    for k in range(8):
+        for h in range(4):
+            send[k, h * T : (h + 1) * T] = got[h, :T]
+        rows = slice(k * 8, k * 8 + 8)
+        send[k, 4 * T :] = jnp.concatenate([high[rows], low[rows]], 0).astype(BF)
 
 
 def backward_kernel(places, count, tiles, got, keep, send, term, acc):
@@ -104,15 +107,16 @@
 
     def load(s):
         row = places[0, s]
-        return got[row // 8, pl.ds(pl.multiple_of((row % 8) * T, T), T)]
+        at = (row % 8) // 2 * T
+        return got[row // 8 * 2 + row % 2, pl.ds(pl.multiple_of(at, T), T)]
 
     block_products(count, tiles, acc, lambda s: places[1, s], load, 0)
     for z in range(8):
         keep[z] = acc[2 * z + core].astype(BF)
         send[z * T : (z + 1) * T] = acc[2 * z + 1 - core].astype(BF)
-    total = got[0, 8 * T :].astype(F32)
-    for k in range(1, 4):
-        total += got[k, 8 * T :].astype(F32)
+    total = got[0, 4 * T :].astype(F32)
+    for k in range(1, 8):
+        total += got[k, 4 * T :].astype(F32)
     total = total[:8] + total[8:]
     term[...] = total
     high = total.astype(BF).astype(F32)
@@ -148,19 +152,19 @@
     own = lax.all_to_all(jnp.broadcast_to(own_rows, (8, T, 256)), "z", 0, 0)
     other = lax.ppermute(own, "c", swap)
     partial = call(
-        forward_kernel, shape((4, 8 * T, 256)), [SM, SM, VM, VM, VM],
+        forward_kernel, shape((8, 4 * T, 256)), [SM, SM, VM, VM, VM],
         places, tile_count, tiles, own, other, scratch=[pltpu.VMEM((32, T, 256), F32)],
     )
-    parts = lax.all_to_all(partial, "x", 0, 0)
-    parts = call(sum_kernel, shape((8 * T, 256)), [VM], parts)
-    parts = lax.all_to_all(parts.reshape(8, T, 256), "y", 0, 0)
+    parts = lax.all_to_all(partial, ("x", "yl"), 0, 0)
+    parts = call(sum_kernel, shape((4 * T, 256)), [VM], parts)
+    parts = lax.all_to_all(parts.reshape(4, T, 256), "yh", 0, 0)
     act, send = call(
-        node_kernel, (shape((T, 256)), shape((8, T + 32, 256))), [VM, VM, VM],
+        node_kernel, (shape((T, 256)), shape((4, T + 64, 256))), [VM, VM, VM],
         parts, weight, upstream[0],
     )
-    got = lax.all_to_all(send, "y", 0, 0)
-    send = call(spread_kernel, shape((4, 8 * T + 16, 256)), [VM], got)
-    got = lax.all_to_all(send, "x", 0, 0)
+    got = lax.all_to_all(send, "yh", 0, 0)
+    send = call(spread_kernel, shape((8, 4 * T + 16, 256)), [VM], got)
+    got = lax.all_to_all(send, ("x", "yl"), 0, 0)
     keep, send, term = call(
         backward_kernel, (shape((8, T, 256)), shape((8 * T + 16, 256)), shape((8, 256), F32)),
         [SM, SM, VM, VM], places, tile_count, tiles, got,
@@ -170,13 +174,13 @@
     send = call(join_kernel, shape((8, T + 16, 256)), [VM, VM, VM], keep, got, term)
     got = lax.all_to_all(send, "z", 0, 0)
     grad, term = call(last_kernel, (shape((T, 256)), shape((32, 8, 256), F32)), [VM], got)
-    grad_weight = lax.all_to_all(term, ("x", "y"), 0, 0)
+    grad_weight = lax.all_to_all(term, ("x", "yh", "yl"), 0, 0)
     return act[None], grad[None], grad_weight.reshape(256, 256)
 
 
 def solution(mesh):
-    fine = Mesh(mesh.devices.reshape(4, 8, 8, 2), ("x", "y", "z", "c"))
-    row, col = ("x", "y"), ("z", "c")
+    fine = Mesh(mesh.devices.reshape(4, 4, 2, 8, 2), ("x", "yh", "yl", "z", "c"))
+    row, col = ("x", "yh", "yl"), ("z", "c")
     placed = (
         P(row, col, None),
         P(),

time: 189 us -> 179 us (0.947)
  blocking collectives: 164 us -> 152 us
    all_to_all x5, blocking collectives: 114 us -> 103 us  [the longest x1 31.9 us: per_device(): parts = lax.all_to_all(partial, ('x', 'yl'), 0, 0)]
where the time goes in v3:
time: 179 us; the launch traced here: 176 us
  blocking collectives  152 us (85%)
  starting transfers between devices  11.7 us (7%)
  Pallas kernels  5.92 us (3%)
  local copies, waits for them, and re-layouts  2.39 us (1%)
  waiting for transfers between devices  2.39 us (1%)
    all_to_all x1, blocking collectives, per_device(): parts = lax.all_to_all(partial, ('x', 'yl'), 0, 0)  31.9 us
    all_to_all x1, blocking collectives, per_device(): got = lax.all_to_all(send, ('x', 'yl'), 0, 0)  29 us
    all_to_all x1, blocking collectives, per_device(): own = lax.all_to_all(jnp.broadcast_to(own_rows, (8, T, 256)), 'z', 0, 0)  26.8 us
    all_to_all x1, blocking collectives, per_device(): got = lax.all_to_all(send, 'z', 0, 0)  22.6 us
    all_to_all x1, blocking collectives, per_device(): grad_weight = lax.all_to_all(term, ('x', 'yh', 'yl'), 0, 0)  15.8 us
    all_to_all x1, blocking collectives, per_device(): parts = lax.all_to_all(parts.reshape(4, T, 256), 'yh', 0, 0)  13.7 us
    all_to_all x1, blocking collectives, per_device(): got = lax.all_to_all(send, 'yh', 0, 0)  12.5 us
    ppermute x1, starting transfers between devices, per_device(): got = lax.ppermute(send, 'c', swap)  7.51 us
  transfers between devices with their start and end apart: 2, of which 2 were waited for; matrix products, arithmetic and copies ran while one was open for 0% of the time, Pallas kernels for 0%

profile of v3, /device:TPU:1, one launch (start us, length us, event | category | flops | bytes accessed | tf_op | source)
XLA Modules:
  0.0 176.0 jit_solution(4798549272131484473)
XLA Ops:
  0.6 0.0 copy-start
  0.6 1.0 broadcast_in_dim.9
  1.6 26.8 %all_to_all.35.own = bf16[8,128,256]{2,1,0:T(8,128)(2,1)S(1)} all-to-all(bf16[8,128,256]{2,1,0:T(8,128)(2,1)S(1)} %broadcast_in_dim.9), channel_id=1, replica_groups=mesh['x'=4,'yh'=4,'yl'=2,'z'=8,'c'=2] {'z'}, dimensions={0} | all-to-all | bytes 1048576 | tf_op jit(solution)/shard_map/all_to_all | solution.py:152
  28.4 4.2 %collective-permute-start = (bf16[8,128,256]{2,1,0:T(8,128)(2,1)S(1)}, bf16[8,128,256]{2,1,0:T(8,128)(2,1)S(1)}, u32[]{:S(2)}, u32[]{:S(2)}) collective-permute-start(bf16[8,128,256]{2,1,0:T(8,128)(2,1)S(1)} %all_to_all.35.own), channel_id=1, source_target_pairs={{0,1},{1,0},{2,3},{3,2},{4,5},{5,4},{6,7},{7,6},{8,9},{9,8},{10,11... | collective-permute-start | bytes 1572872 | tf_op jit(solution)/shard_map/ppermute | solution.py:153
  33.3 0.9 collective-permute-done.other
  34.2 0.0 copy-done
  34.2 0.0 copy-start.3
  34.2 0.7 copy-done.3
  34.8 2.0 %shard_map.85 = bf16[8,512,256]{2,1,0:T(8,128)(2,1)S(1)} custom-call(s32[2,48]{1,0:T(2,128)S(1)} %bitcast.12, s32[1,1]{1,0:T(1,128)S(6)} %copy.10.count, bf16[48,128,128]{2,1,0:T(8,128)(2,1)S(1)} %bitcast.8, bf16[8,128,256]{2,1,0:T(8,128)(2,1)S(1)} %all_to_all.35.own, bf16[8,128,256]{2,1,0:T(8,128)(2,1)S(1)} %collective-permute-done.other), custom_call_target="tpu_custom_call" | custom-call | tf_op jit(solution)/shard_map/pallas_call | solution.py:17
  36.8 31.9 %all_to_all.36.parts = bf16[8,512,256]{2,1,0:T(8,128)(2,1)S(1)} all-to-all(bf16[8,512,256]{2,1,0:T(8,128)(2,1)S(1)} %shard_map.85), channel_id=1, replica_groups=mesh['x'=4,'yh'=4,'yl'=2,'z'=8,'c'=2] {'x','yl'}, dimensions={0} | all-to-all | bytes 4194304 | tf_op jit(solution)/shard_map/all_to_all | solution.py:158
  68.7 0.0 copy-start.1
  68.7 0.0 copy-start.2
  68.7 0.3 shard_map.86
  69.0 13.7 %all_to_all.37.parts = bf16[4,128,256]{2,1,0:T(8,128)(2,1)S(1)} all-to-all(bf16[4,128,256]{2,1,0:T(8,128)(2,1)S(1)} %bitcast.10), channel_id=1, replica_groups=mesh['x'=4,'yh'=4,'yl'=2,'z'=8,'c'=2] {'yh'}, dimensions={0} | all-to-all | bytes 524288 | tf_op jit(solution)/shard_map/all_to_all | solution.py:160
  82.7 0.0 copy-done.1
  82.7 0.0 copy-done.2
  82.7 0.8 shard_map.87
  83.5 12.5 %all_to_all.38.got = bf16[4,192,256]{2,1,0:T(8,128)(2,1)S(1)} all-to-all(bf16[4,192,256]{2,1,0:T(8,128)(2,1)S(1)} %get-tuple-element.11), channel_id=1, replica_groups=mesh['x'=4,'yh'=4,'yl'=2,'z'=8,'c'=2] {'yh'}, dimensions={0} | all-to-all | bytes 786432 | tf_op jit(solution)/shard_map/all_to_all | solution.py:165
  96.0 0.1 shard_map.88
  96.2 0.0 copy-start.4
  96.2 29.0 %all_to_all.39.got = bf16[8,528,256]{2,1,0:T(8,128)(2,1)S(1)} all-to-all(bf16[8,528,256]{2,1,0:T(8,128)(2,1)S(1)} %shard_map.88), channel_id=1, replica_groups=mesh['x'=4,'yh'=4,'yl'=2,'z'=8,'c'=2] {'x','yl'}, dimensions={0} | all-to-all | bytes 4325376 | tf_op jit(solution)/shard_map/all_to_all | solution.py:167
  125.2 0.0 copy-done.4
  125.2 1.9 %shard_map.89 = (bf16[8,128,256]{2,1,0:T(8,128)(2,1)S(1)}, bf16[1040,256]{1,0:T(8,128)(2,1)S(1)}, f32[8,256]{1,0:T(8,128)S(1)}) custom-call(s32[2,48]{1,0:T(2,128)S(1)} %bitcast.13, s32[1,1]{1,0:T(1,128)S(6)} %copy.10.count, bf16[48,128,128]{2,1,0:T(8,128)(2,1)S(1)} %bitcast.9, bf16[8,528,256]{2,1,0:T(8,128)(2,1)S(1)} %all_to_all.39.got), custom_call_target="tpu_custom_call" | custom-call | tf_op jit(solution)/shard_map/pallas_call | solution.py:17
  127.1 7.5 %collective-permute-start.1 = (bf16[1040,256]{1,0:T(8,128)(2,1)S(1)}, bf16[1040,256]{1,0:T(8,128)(2,1)S(1)}, u32[]{:S(2)}, u32[]{:S(2)}) collective-permute-start(bf16[1040,256]{1,0:T(8,128)(2,1)S(1)} %get-tuple-element.13), channel_id=1, source_target_pairs={{0,1},{1,0},{2,3},{3,2},{4,5},{5,4},{6,7},{7,6},{8,9},{9,8},{10,11... | collective-permute-start | bytes 1597448 | tf_op jit(solution)/shard_map/ppermute | solution.py:173
  134.6 1.5 collective-permute-done.1.got
  136.1 0.1 shard_map.90
  136.2 22.6 %all_to_all.40.got = bf16[8,144,256]{2,1,0:T(8,128)(2,1)S(1)} all-to-all(bf16[8,144,256]{2,1,0:T(8,128)(2,1)S(1)} %shard_map.90), channel_id=1, replica_groups=mesh['x'=4,'yh'=4,'yl'=2,'z'=8,'c'=2] {'z'}, dimensions={0} | all-to-all | bytes 1179648 | tf_op jit(solution)/shard_map/all_to_all | solution.py:175
  158.9 0.7 shard_map.91
  159.6 15.8 %all_to_all.41 = f32[32,8,256]{2,1,0:T(8,128)S(1)} all-to-all(f32[32,8,256]{2,1,0:T(8,128)S(1)} %get-tuple-element.16), channel_id=1, replica_groups=mesh['x'=4,'yh'=4,'yl'=2,'z'=8,'c'=2] {'x','yh','yl'}, dimensions={0} | all-to-all | bytes 524288 | tf_op jit(solution)/shard_map/all_to_all | solution.py:177
  175.3 0.7 copy.11
Async XLA Ops:
  0.6 33.5 %copy-start = (bf16[1,1,48,128,128]{4,3,2,1,0:T(8,128)(2,1)S(1)}, bf16[1,1,48,128,128]{4,3,2,1,0:T(8,128)(2,1)}, u32[]{:S(2)}) copy-start(bf16[1,1,48,128,128]{4,3,2,1,0:T(8,128)(2,1)} %param.8) | copy-start | bytes 4718596
  28.4 5.8 %collective-permute-start = (bf16[8,128,256]{2,1,0:T(8,128)(2,1)S(1)}, bf16[8,128,256]{2,1,0:T(8,128)(2,1)S(1)}, u32[]{:S(2)}, u32[]{:S(2)}) collective-permute-start(bf16[8,128,256]{2,1,0:T(8,128)(2,1)S(1)} %all_to_all.35.own), channel_id=1, source_target_pairs={{0,1},{1,0},{2,3},{3,2},{4,5},{5,4},{6,7},{7,6},{8,9},{9,8},{10,11... | collective-permute-start | bytes 1572872 | tf_op jit(solution)/shard_map/ppermute | solution.py:153
  34.2 0.7 copy-start.3
  68.7 14.0 %copy-start.1 = (bf16[256,256]{1,0:T(8,128)(2,1)S(1)}, bf16[256,256]{1,0:T(8,128)(2,1)}, u32[]{:S(2)}) copy-start(bf16[256,256]{1,0:T(8,128)(2,1)} %weight.1) | copy-start | bytes 393220
  68.7 14.0 %copy-start.2 = (bf16[1,128,256]{2,1,0:T(8,128)(2,1)S(1)}, bf16[1,128,256]{2,1,0:T(8,128)(2,1)}, u32[]{:S(2)}) copy-start(bf16[1,128,256]{2,1,0:T(8,128)(2,1)} %param.11) | copy-start | bytes 196612
  96.2 29.0 %copy-start.4 = (s32[1,1,2,48]{3,2,1,0:T(2,128)S(1)}, s32[1,1,2,48]{3,2,1,0:T(2,128)}, u32[]{:S(2)}) copy-start(s32[1,1,2,48]{3,2,1,0:T(2,128)} %param.9) | copy-start | bytes 1156
  127.1 9.0 %collective-permute-start.1 = (bf16[1040,256]{1,0:T(8,128)(2,1)S(1)}, bf16[1040,256]{1,0:T(8,128)(2,1)S(1)}, u32[]{:S(2)}, u32[]{:S(2)}) collective-permute-start(bf16[1040,256]{1,0:T(8,128)(2,1)S(1)} %get-tuple-element.13), channel_id=1, source_target_pairs={{0,1},{1,0},{2,3},{3,2},{4,5},{5,4},{6,7},{7,6},{8,9},{9,8},{10,11... | collective-permute-start | bytes 1597448 | tf_op jit(solution)/shard_map/ppermute | solution.py:173

commit v4 on v3

--- a/solution.py
+++ b/solution.py
@@ -62,44 +62,51 @@
         out[row // 8 * 2 + row % 2, at : at + T] = acc[row].astype(BF)
 
 
-def sum_kernel(parts, out):
-    total = parts[0].astype(F32)
-    for k in range(1, parts.shape[0]):
-        total += parts[k].astype(F32)
-    out[...] = total.astype(BF)
-
-
-def node_kernel(parts, weight, upstream, act, send):
-    agg = parts[0].astype(F32)
-    for k in range(1, parts.shape[0]):
-        agg += parts[k].astype(F32)
+def fold_kernel(parts, *outs):
+    me = lax.axis_index("yh")
+    for k in range(4):
+        at = pl.multiple_of((me + k) % 4 * T, T)
+        total = parts[0, pl.ds(at, T)].astype(F32)
+        for j in range(1, 8):
+            total += parts[j, pl.ds(at, T)].astype(F32)
+        outs[k][...] = total.astype(BF)
+
+
+def node_kernel(mine, one, two, three, weight, upstream, act, back, term):
+    agg = (mine[...].astype(F32) + one[...].astype(F32)) + (
+        two[...].astype(F32) + three[...].astype(F32)
+    )
     agg = agg.astype(BF)
     pre = jnp.dot(agg, weight[...], preferred_element_type=F32)
     sigma = jax.nn.sigmoid(pre)
     act[...] = (pre * sigma).astype(BF)
     slope = (upstream[...].astype(F32) * sigma * (1.0 + pre * (1.0 - sigma))).astype(BF)
-    back = lax.dot_general(
+    back[...] = lax.dot_general(
         slope, weight[...], (((1,), (1,)), ((), ())), preferred_element_type=F32
     ).astype(BF)
-    term = lax.dot_general(agg, slope, (((0,), (0,)), ((), ())), preferred_element_type=F32)
-    for h in range(4):
-        send[h, :T] = back
-        for x in range(4):
-            at = x * 64 + h * 16
-            send[h, T + x * 16 : T + x * 16 + 16] = term[at : at + 16].astype(BF)
-
-
-def spread_kernel(got, send):
-    term = got[0, T:].astype(F32)
-    for k in range(1, 4):
-        term += got[k, T:].astype(F32)
-    high = term.astype(BF).astype(F32)
-    low = term - high
-    for k in range(8):
-        for h in range(4):
-            send[k, h * T : (h + 1) * T] = got[h, :T]
-        rows = slice(k * 8, k * 8 + 8)
-        send[k, 4 * T :] = jnp.concatenate([high[rows], low[rows]], 0).astype(BF)
+    product = lax.dot_general(agg, slope, (((0,), (0,)), ((), ())), preferred_element_type=F32)
+    term[...] = product.astype(BF).reshape(8, 32, 256)
+
+
+def pack_kernel(back, got, send):
+    send[:T] = back[...]
+    term = got[0].astype(F32)
+    for k in range(1, 8):
+        term += got[k].astype(F32)
+    send[T:] = term.astype(BF)
+
+
+def spread_kernel(mine, one, two, three, send, terms):
+    me = lax.axis_index("yh")
+    for k, part in enumerate((mine, one, two, three)):
+        h = (me + 4 - k) % 4
+        terms[h] = part[T:].astype(F32)
+        at = pl.multiple_of(h * T, T)
+        for j in range(8):
+            send[j, pl.ds(at, T)] = part[:T]
+    total = ((terms[0] + terms[1]) + (terms[2] + terms[3])).astype(BF)
+    for j in range(8):
+        send[j, 4 * T :] = total
 
 
 def backward_kernel(places, count, tiles, got, keep, send, term, acc):
@@ -117,30 +124,34 @@
     total = got[0, 4 * T :].astype(F32)
     for k in range(1, 8):
         total += got[k, 4 * T :].astype(F32)
-    total = total[:8] + total[8:]
     term[...] = total
-    high = total.astype(BF).astype(F32)
-    send[8 * T :] = jnp.concatenate([high, total - high], 0).astype(BF)
+    high = total.astype(BF)
+    send[8 * T : 8 * T + 32] = high
+    send[8 * T + 32 :] = (total - high.astype(F32)).astype(BF)
 
 
 def join_kernel(keep, got, term, send):
-    other = got[8 * T :].astype(F32)
-    total = term[...] + (other[:8] + other[8:])
-    high = total.astype(BF).astype(F32)
-    both = jnp.concatenate([high, total - high], 0).astype(BF)
+    other = got[8 * T : 8 * T + 32].astype(F32) + got[8 * T + 32 :].astype(F32)
+    mine = term[...]
+    high = mine.astype(BF).astype(F32)
+    mine = high + (mine - high).astype(BF).astype(F32)
+    both = (mine + other).astype(BF)
     for z in range(8):
         send[z, :T] = (keep[z].astype(F32) + got[z * T : (z + 1) * T].astype(F32)).astype(BF)
         send[z, T:] = both
 
 
 def last_kernel(got, grad, term):
-    total = got[0].astype(F32)
+    total = got[0, :T].astype(F32)
     for k in range(1, 8):
-        total += got[k].astype(F32)
-    grad[...] = total[:T].astype(BF)
-    rows = total[T : T + 8] + total[T + 8 :]
-    for k in range(32):
-        term[k] = rows
+        total += got[k, :T].astype(F32)
+    grad[...] = total.astype(BF)
+    for k in range(8):
+        term[k * 32 : k * 32 + 32] = got[k, T:].astype(F32)
+
+
+def shifted(value, by):
+    return lax.ppermute(value, "yh", [(i, (i + by) % 4) for i in range(4)])
 
 
 def per_device(features, weight, tile_values, tile_places, tile_count, upstream):
@@ -156,26 +167,30 @@
         places, tile_count, tiles, own, other, scratch=[pltpu.VMEM((32, T, 256), F32)],
     )
     parts = lax.all_to_all(partial, ("x", "yl"), 0, 0)
-    parts = call(sum_kernel, shape((4 * T, 256)), [VM], parts)
-    parts = lax.all_to_all(parts.reshape(4, T, 256), "yh", 0, 0)
-    act, send = call(
-        node_kernel, (shape((T, 256)), shape((4, T + 64, 256))), [VM, VM, VM],
-        parts, weight, upstream[0],
-    )
-    got = lax.all_to_all(send, "yh", 0, 0)
-    send = call(spread_kernel, shape((8, 4 * T + 16, 256)), [VM], got)
+    parts = call(fold_kernel, (shape((T, 256)),) * 4, [VM], parts)
+    parts = [parts[0]] + [shifted(parts[k], k) for k in (1, 2, 3)]
+    act, back, term = call(
+        node_kernel, (shape((T, 256)), shape((T, 256)), shape((8, 32, 256))), [VM] * 6,
+        *parts, weight, upstream[0],
+    )
+    term = lax.all_to_all(term, "z", 0, 0)
+    send = call(pack_kernel, shape((T + 32, 256)), [VM, VM], back, term)
+    sends = [send] + [shifted(send, k) for k in (1, 2, 3)]
+    send = call(
+        spread_kernel, shape((8, 4 * T + 32, 256)), [VM] * 4, *sends,
+        scratch=[pltpu.VMEM((4, 32, 256), F32)],
+    )
     got = lax.all_to_all(send, ("x", "yl"), 0, 0)
     keep, send, term = call(
-        backward_kernel, (shape((8, T, 256)), shape((8 * T + 16, 256)), shape((8, 256), F32)),
+        backward_kernel, (shape((8, T, 256)), shape((8 * T + 64, 256)), shape((32, 256), F32)),
         [SM, SM, VM, VM], places, tile_count, tiles, got,
         scratch=[pltpu.VMEM((16, T, 256), F32)],
     )
     got = lax.ppermute(send, "c", swap)
-    send = call(join_kernel, shape((8, T + 16, 256)), [VM, VM, VM], keep, got, term)
+    send = call(join_kernel, shape((8, T + 32, 256)), [VM, VM, VM], keep, got, term)
     got = lax.all_to_all(send, "z", 0, 0)
-    grad, term = call(last_kernel, (shape((T, 256)), shape((32, 8, 256), F32)), [VM], got)
-    grad_weight = lax.all_to_all(term, ("x", "yh", "yl"), 0, 0)
-    return act[None], grad[None], grad_weight.reshape(256, 256)
+    grad, grad_weight = call(last_kernel, (shape((T, 256)), shape((256, 256), F32)), [VM], got)
+    return act[None], grad[None], grad_weight
 
 
 def solution(mesh):

time: 179 us -> 181 us (1.011); the launches traced: 176 us -> 180 us
  blocking collectives: 152 us -> 118 us
  starting transfers between devices: 11.7 us -> 41.3 us
  waiting for transfers between devices: 2.39 us -> 11.8 us
    all_to_all x3 -> x1, blocking collectives: 42 us -> 10.3 us  [per_device(): term = lax.all_to_all(term, 'z', 0, 0)]
    ppermute x0 -> x6, starting transfers between devices: none -> 29.2 us  [shifted(): return lax.ppermute(value, 'yh', [(i, (i + by) % 4) for i in range(4)])]
    ppermute x0 -> x6, waiting for transfers between devices: none -> 9.4 us  [shifted(): return lax.ppermute(value, 'yh', [(i, (i + by) % 4) for i in range(4)])]
    pallas_call x7 -> x8, Pallas kernels: 5.92 us -> 6.58 us  [call(): pl.pallas_call(kernel, out_shape=outs, in_specs=in_specs, out_specs=jax.t...]
  transfers between devices with their start and end apart: 2 -> 8, of which waited for: 2 -> 6; matrix products, arithmetic and copies ran while one was open for 0% -> 0% of each run, Pallas kernels for 0% -> 0%
where the time goes in v4:
time: 181 us; the launch traced here: 180 us
  blocking collectives  118 us (65%)
  starting transfers between devices  41.3 us (23%)
  waiting for transfers between devices  11.8 us (7%)
  Pallas kernels  6.58 us (4%)
    all_to_all x1, blocking collectives, per_device(): parts = lax.all_to_all(partial, ('x', 'yl'), 0, 0)  30.7 us
    ppermute x6, starting transfers between devices, shifted(): return lax.ppermute(value, 'yh', [(i, (i + by) % 4) for i in range(4)])  29.2 us
    all_to_all x1, blocking collectives, per_device(): got = lax.all_to_all(send, ('x', 'yl'), 0, 0)  27.7 us
    all_to_all x1, blocking collectives, per_device(): own = lax.all_to_all(jnp.broadcast_to(own_rows, (8, T, 256)), 'z', 0, 0)  26.8 us
    all_to_all x1, blocking collectives, per_device(): got = lax.all_to_all(send, 'z', 0, 0)  22.2 us
    all_to_all x1, blocking collectives, per_device(): term = lax.all_to_all(term, 'z', 0, 0)  10.3 us
    ppermute x6, waiting for transfers between devices, shifted(): return lax.ppermute(value, 'yh', [(i, (i + by) % 4) for i in range(4)])  9.4 us
    ppermute x1, starting transfers between devices, per_device(): got = lax.ppermute(send, 'c', swap)  7.9 us
  transfers between devices with their start and end apart: 8, of which 6 were waited for; matrix products, arithmetic and copies ran while one was open for 0% of the time, Pallas kernels for 0%

profile of v4, /device:TPU:1, one launch (start us, length us, event | category | flops | bytes accessed | tf_op | source)
XLA Modules:
  0.0 180.4 jit_solution(1963940304085484019)
XLA Ops:
  0.6 1.0 broadcast_in_dim.9
  1.6 26.8 %all_to_all.25.own = bf16[8,128,256]{2,1,0:T(8,128)(2,1)S(1)} all-to-all(bf16[8,128,256]{2,1,0:T(8,128)(2,1)S(1)} %broadcast_in_dim.9), channel_id=1, replica_groups=mesh['x'=4,'yh'=4,'yl'=2,'z'=8,'c'=2] {'z'}, dimensions={0} | all-to-all | bytes 1048576 | tf_op jit(solution)/shard_map/all_to_all | solution.py:163
  28.4 4.2 %collective-permute-start = (bf16[8,128,256]{2,1,0:T(8,128)(2,1)S(1)}, bf16[8,128,256]{2,1,0:T(8,128)(2,1)S(1)}, u32[]{:S(2)}, u32[]{:S(2)}) collective-permute-start(bf16[8,128,256]{2,1,0:T(8,128)(2,1)S(1)} %all_to_all.25.own), channel_id=1, source_target_pairs={{0,1},{1,0},{2,3},{3,2},{4,5},{5,4},{6,7},{7,6},{8,9},{9,8},{10,11... | collective-permute-start | bytes 1572872 | tf_op jit(solution)/shard_map/ppermute | solution.py:164
  33.3 0.9 collective-permute-done.other
  34.2 0.7 copy-done.3
  34.8 2.2 %shard_map.85 = bf16[8,512,256]{2,1,0:T(8,128)(2,1)S(1)} custom-call(s32[2,48]{1,0:T(2,128)S(1)} %bitcast.9, s32[1,1]{1,0:T(1,128)S(6)} %copy.9.count, bf16[48,128,128]{2,1,0:T(8,128)(2,1)S(1)} %bitcast.6, bf16[8,128,256]{2,1,0:T(8,128)(2,1)S(1)} %all_to_all.25.own, bf16[8,128,256]{2,1,0:T(8,128)(2,1)S(1)} %collective-permute-done.other), custom_call_target="tpu_custom_call" | custom-call | tf_op jit(solution)/shard_map/pallas_call | solution.py:17
  37.1 30.7 %all_to_all.26.parts = bf16[8,512,256]{2,1,0:T(8,128)(2,1)S(1)} all-to-all(bf16[8,512,256]{2,1,0:T(8,128)(2,1)S(1)} %shard_map.85), channel_id=1, replica_groups=mesh['x'=4,'yh'=4,'yl'=2,'z'=8,'c'=2] {'x','yl'}, dimensions={0} | all-to-all | bytes 4194304 | tf_op jit(solution)/shard_map/all_to_all | solution.py:169
  67.8 0.3 shard_map.86
  68.0 6.7 %collective-permute-start.1 = (bf16[128,256]{1,0:T(8,128)(2,1)S(1)}, bf16[128,256]{1,0:T(8,128)(2,1)S(1)}, u32[]{:S(2)}, u32[]{:S(2)}) collective-permute-start(bf16[128,256]{1,0:T(8,128)(2,1)S(1)} %get-tuple-element.16), channel_id=1, source_target_pairs={{0,32},{32,64},{64,96},{96,0},{1,33},{33,65},{65,97},{97,1},{2,34}... | collective-permute-start | bytes 196616 | tf_op jit(solution)/shard_map/ppermute | solution.py:154
  74.8 4.2 %collective-permute-start.2 = (bf16[128,256]{1,0:T(8,128)(2,1)S(1)}, bf16[128,256]{1,0:T(8,128)(2,1)S(1)}, u32[]{:S(2)}, u32[]{:S(2)}) collective-permute-start(bf16[128,256]{1,0:T(8,128)(2,1)S(1)} %get-tuple-element.17), channel_id=1, source_target_pairs={{0,64},{32,96},{64,0},{96,32},{1,65},{33,97},{65,1},{97,33},{2,66}... | collective-permute-start | bytes 196616 | tf_op jit(solution)/shard_map/ppermute | solution.py:154
  79.0 5.5 %collective-permute-start.3 = (bf16[128,256]{1,0:T(8,128)(2,1)S(1)}, bf16[128,256]{1,0:T(8,128)(2,1)S(1)}, u32[]{:S(2)}, u32[]{:S(2)}) collective-permute-start(bf16[128,256]{1,0:T(8,128)(2,1)S(1)} %get-tuple-element.18), channel_id=1, source_target_pairs={{0,96},{32,0},{64,32},{96,64},{1,97},{33,1},{65,33},{97,65},{2,98}... | collective-permute-start | bytes 196616 | tf_op jit(solution)/shard_map/ppermute | solution.py:154
  84.5 0.0 collective-permute-done.1.one
  84.5 0.1 collective-permute-done.2.two
  84.6 2.6 %collective-permute-done.3.three = bf16[128,256]{1,0:T(8,128)(2,1)S(1)} collective-permute-done((bf16[128,256]{1,0:T(8,128)(2,1)S(1)}, bf16[128,256]{1,0:T(8,128)(2,1)S(1)}, u32[]{:S(2)}, u32[]{:S(2)}) %collective-permute-start.3) | collective-permute-done | bytes 65568 | tf_op jit(solution)/shard_map/ppermute | solution.py:154
  87.2 0.0 copy-done.1
  87.2 0.8 shard_map.87
  88.0 10.3 %all_to_all.27.got = bf16[8,32,256]{2,1,0:T(8,128)(2,1)S(1)} all-to-all(bf16[8,32,256]{2,1,0:T(8,128)(2,1)S(1)} %get-tuple-element.21), channel_id=1, replica_groups=mesh['x'=4,'yh'=4,'yl'=2,'z'=8,'c'=2] {'z'}, dimensions={0} | all-to-all | bytes 262144 | tf_op jit(solution)/shard_map/all_to_all | solution.py:176
  98.3 6.2 %collective-permute-start.6 = (bf16[160,256]{1,0:T(8,128)(2,1)S(1)}, bf16[160,256]{1,0:T(8,128)(2,1)S(1)}, u32[]{:S(2)}, u32[]{:S(2)}) collective-permute-start(bf16[160,256]{1,0:T(8,128)(2,1)S(1)} %shard_map.88.mine), channel_id=1, source_target_pairs={{0,96},{32,0},{64,32},{96,64},{1,97},{33,1},{65,33},{97,65},{2,98}... | collective-permute-start | bytes 245768 | tf_op jit(solution)/shard_map/ppermute | solution.py:154
  104.5 4.6 %collective-permute-start.5 = (bf16[160,256]{1,0:T(8,128)(2,1)S(1)}, bf16[160,256]{1,0:T(8,128)(2,1)S(1)}, u32[]{:S(2)}, u32[]{:S(2)}) collective-permute-start(bf16[160,256]{1,0:T(8,128)(2,1)S(1)} %shard_map.88.mine), channel_id=1, source_target_pairs={{0,64},{32,96},{64,0},{96,32},{1,65},{33,97},{65,1},{97,33},{2,66}... | collective-permute-start | bytes 245768 | tf_op jit(solution)/shard_map/ppermute | solution.py:154
  109.2 1.9 %collective-permute-start.4 = (bf16[160,256]{1,0:T(8,128)(2,1)S(1)}, bf16[160,256]{1,0:T(8,128)(2,1)S(1)}, u32[]{:S(2)}, u32[]{:S(2)}) collective-permute-start(bf16[160,256]{1,0:T(8,128)(2,1)S(1)} %shard_map.88.mine), channel_id=1, source_target_pairs={{0,32},{32,64},{64,96},{96,0},{1,33},{33,65},{65,97},{97,1},{2,34}... | collective-permute-start | bytes 245768 | tf_op jit(solution)/shard_map/ppermute | solution.py:154
  111.1 0.0 collective-permute-done.6.three
  111.1 3.5 %collective-permute-done.5.two = bf16[160,256]{1,0:T(8,128)(2,1)S(1)} collective-permute-done((bf16[160,256]{1,0:T(8,128)(2,1)S(1)}, bf16[160,256]{1,0:T(8,128)(2,1)S(1)}, u32[]{:S(2)}, u32[]{:S(2)}) %collective-permute-start.5) | collective-permute-done | bytes 81952 | tf_op jit(solution)/shard_map/ppermute | solution.py:154
  114.6 3.2 %collective-permute-done.4.one = bf16[160,256]{1,0:T(8,128)(2,1)S(1)} collective-permute-done((bf16[160,256]{1,0:T(8,128)(2,1)S(1)}, bf16[160,256]{1,0:T(8,128)(2,1)S(1)}, u32[]{:S(2)}, u32[]{:S(2)}) %collective-permute-start.4) | collective-permute-done | bytes 81952 | tf_op jit(solution)/shard_map/ppermute | solution.py:154
  117.8 0.2 shard_map.89
  118.0 0.0 copy-start.4
  118.0 27.7 %all_to_all.28.got = bf16[8,544,256]{2,1,0:T(8,128)(2,1)S(1)} all-to-all(bf16[8,544,256]{2,1,0:T(8,128)(2,1)S(1)} %shard_map.89), channel_id=1, replica_groups=mesh['x'=4,'yh'=4,'yl'=2,'z'=8,'c'=2] {'x','yl'}, dimensions={0} | all-to-all | bytes 4456448 | tf_op jit(solution)/shard_map/all_to_all | solution.py:183
  145.7 2.1 %shard_map.90 = (bf16[8,128,256]{2,1,0:T(8,128)(2,1)S(1)}, bf16[1088,256]{1,0:T(8,128)(2,1)S(1)}, f32[32,256]{1,0:T(8,128)S(1)}) custom-call(s32[2,48]{1,0:T(2,128)S(1)} %bitcast.10, s32[1,1]{1,0:T(1,128)S(6)} %copy.9.count, bf16[48,128,128]{2,1,0:T(8,128)(2,1)S(1)} %bitcast.7, bf16[8,544,256]{2,1,0:T(8,128)(2,1)S(1)} %all_to_all.28.got), custom_call_target="tpu_custom_call" | custom-call | tf_op jit(solution)/shard_map/pallas_call | solution.py:17
  147.8 7.9 %collective-permute-start.7 = (bf16[1088,256]{1,0:T(8,128)(2,1)S(1)}, bf16[1088,256]{1,0:T(8,128)(2,1)S(1)}, u32[]{:S(2)}, u32[]{:S(2)}) collective-permute-start(bf16[1088,256]{1,0:T(8,128)(2,1)S(1)} %get-tuple-element.23), channel_id=1, source_target_pairs={{0,1},{1,0},{2,3},{3,2},{4,5},{5,4},{6,7},{7,6},{8,9},{9,8},{10,11... | collective-permute-start | bytes 1671176 | tf_op jit(solution)/shard_map/ppermute | solution.py:189
  155.7 1.6 collective-permute-done.7.got
  157.3 0.1 shard_map.91
  157.4 22.2 %all_to_all.29.got = bf16[8,160,256]{2,1,0:T(8,128)(2,1)S(1)} all-to-all(bf16[8,160,256]{2,1,0:T(8,128)(2,1)S(1)} %shard_map.91), channel_id=1, replica_groups=mesh['x'=4,'yh'=4,'yl'=2,'z'=8,'c'=2] {'z'}, dimensions={0} | all-to-all | bytes 1310720 | tf_op jit(solution)/shard_map/all_to_all | solution.py:191
  179.6 0.8 shard_map.92
  (8 shorter events, 0.0 us)
Async XLA Ops:
  0.6 33.5 %copy-start = (bf16[1,1,48,128,128]{4,3,2,1,0:T(8,128)(2,1)S(1)}, bf16[1,1,48,128,128]{4,3,2,1,0:T(8,128)(2,1)}, u32[]{:S(2)}) copy-start(bf16[1,1,48,128,128]{4,3,2,1,0:T(8,128)(2,1)} %param.8) | copy-start | bytes 4718596
  28.4 5.8 %collective-permute-start = (bf16[8,128,256]{2,1,0:T(8,128)(2,1)S(1)}, bf16[8,128,256]{2,1,0:T(8,128)(2,1)S(1)}, u32[]{:S(2)}, u32[]{:S(2)}) collective-permute-start(bf16[8,128,256]{2,1,0:T(8,128)(2,1)S(1)} %all_to_all.25.own), channel_id=1, source_target_pairs={{0,1},{1,0},{2,3},{3,2},{4,5},{5,4},{6,7},{7,6},{8,9},{9,8},{10,11... | collective-permute-start | bytes 1572872 | tf_op jit(solution)/shard_map/ppermute | solution.py:164
  34.2 0.7 copy-start.3
  67.8 19.4 %copy-start.1 = (bf16[256,256]{1,0:T(8,128)(2,1)S(1)}, bf16[256,256]{1,0:T(8,128)(2,1)}, u32[]{:S(2)}) copy-start(bf16[256,256]{1,0:T(8,128)(2,1)} %weight.1) | copy-start | bytes 393220
  67.8 19.4 %copy-start.2 = (bf16[1,128,256]{2,1,0:T(8,128)(2,1)S(1)}, bf16[1,128,256]{2,1,0:T(8,128)(2,1)}, u32[]{:S(2)}) copy-start(bf16[1,128,256]{2,1,0:T(8,128)(2,1)} %param.11) | copy-start | bytes 196612
  68.0 16.4 %collective-permute-start.1 = (bf16[128,256]{1,0:T(8,128)(2,1)S(1)}, bf16[128,256]{1,0:T(8,128)(2,1)S(1)}, u32[]{:S(2)}, u32[]{:S(2)}) collective-permute-start(bf16[128,256]{1,0:T(8,128)(2,1)S(1)} %get-tuple-element.16), channel_id=1, source_target_pairs={{0,32},{32,64},{64,96},{96,0},{1,33},{33,65},{65,97},{97,1},{2,34}... | collective-permute-start | bytes 196616 | tf_op jit(solution)/shard_map/ppermute | solution.py:154
  74.8 9.8 %collective-permute-start.2 = (bf16[128,256]{1,0:T(8,128)(2,1)S(1)}, bf16[128,256]{1,0:T(8,128)(2,1)S(1)}, u32[]{:S(2)}, u32[]{:S(2)}) collective-permute-start(bf16[128,256]{1,0:T(8,128)(2,1)S(1)} %get-tuple-element.17), channel_id=1, source_target_pairs={{0,64},{32,96},{64,0},{96,32},{1,65},{33,97},{65,1},{97,33},{2,66}... | collective-permute-start | bytes 196616 | tf_op jit(solution)/shard_map/ppermute | solution.py:154
  79.0 8.2 %collective-permute-start.3 = (bf16[128,256]{1,0:T(8,128)(2,1)S(1)}, bf16[128,256]{1,0:T(8,128)(2,1)S(1)}, u32[]{:S(2)}, u32[]{:S(2)}) collective-permute-start(bf16[128,256]{1,0:T(8,128)(2,1)S(1)} %get-tuple-element.18), channel_id=1, source_target_pairs={{0,96},{32,0},{64,32},{96,64},{1,97},{33,1},{65,33},{97,65},{2,98}... | collective-permute-start | bytes 196616 | tf_op jit(solution)/shard_map/ppermute | solution.py:154
  98.3 12.8 %collective-permute-start.6 = (bf16[160,256]{1,0:T(8,128)(2,1)S(1)}, bf16[160,256]{1,0:T(8,128)(2,1)S(1)}, u32[]{:S(2)}, u32[]{:S(2)}) collective-permute-start(bf16[160,256]{1,0:T(8,128)(2,1)S(1)} %shard_map.88.mine), channel_id=1, source_target_pairs={{0,96},{32,0},{64,32},{96,64},{1,97},{33,1},{65,33},{97,65},{2,98}... | collective-permute-start | bytes 245768 | tf_op jit(solution)/shard_map/ppermute | solution.py:154
  104.5 10.1 %collective-permute-start.5 = (bf16[160,256]{1,0:T(8,128)(2,1)S(1)}, bf16[160,256]{1,0:T(8,128)(2,1)S(1)}, u32[]{:S(2)}, u32[]{:S(2)}) collective-permute-start(bf16[160,256]{1,0:T(8,128)(2,1)S(1)} %shard_map.88.mine), channel_id=1, source_target_pairs={{0,64},{32,96},{64,0},{96,32},{1,65},{33,97},{65,1},{97,33},{2,66}... | collective-permute-start | bytes 245768 | tf_op jit(solution)/shard_map/ppermute | solution.py:154
  109.2 8.6 %collective-permute-start.4 = (bf16[160,256]{1,0:T(8,128)(2,1)S(1)}, bf16[160,256]{1,0:T(8,128)(2,1)S(1)}, u32[]{:S(2)}, u32[]{:S(2)}) collective-permute-start(bf16[160,256]{1,0:T(8,128)(2,1)S(1)} %shard_map.88.mine), channel_id=1, source_target_pairs={{0,32},{32,64},{64,96},{96,0},{1,33},{33,65},{65,97},{97,1},{2,34}... | collective-permute-start | bytes 245768 | tf_op jit(solution)/shard_map/ppermute | solution.py:154
  118.0 27.7 %copy-start.4 = (s32[1,1,2,48]{3,2,1,0:T(2,128)S(1)}, s32[1,1,2,48]{3,2,1,0:T(2,128)}, u32[]{:S(2)}) copy-start(s32[1,1,2,48]{3,2,1,0:T(2,128)} %param.9) | copy-start | bytes 1156
  147.8 9.5 %collective-permute-start.7 = (bf16[1088,256]{1,0:T(8,128)(2,1)S(1)}, bf16[1088,256]{1,0:T(8,128)(2,1)S(1)}, u32[]{:S(2)}, u32[]{:S(2)}) collective-permute-start(bf16[1088,256]{1,0:T(8,128)(2,1)S(1)} %get-tuple-element.23), channel_id=1, source_target_pairs={{0,1},{1,0},{2,3},{3,2},{4,5},{5,4},{6,7},{7,6},{8,9},{9,8},{10,11... | collective-permute-start | bytes 1671176 | tf_op jit(solution)/shard_map/ppermute | solution.py:189

commit v5 on v4

--- a/solution.py
+++ b/solution.py
@@ -62,20 +62,17 @@
         out[row // 8 * 2 + row % 2, at : at + T] = acc[row].astype(BF)
 
 
-def fold_kernel(parts, *outs):
-    me = lax.axis_index("yh")
-    for k in range(4):
-        at = pl.multiple_of((me + k) % 4 * T, T)
-        total = parts[0, pl.ds(at, T)].astype(F32)
-        for j in range(1, 8):
-            total += parts[j, pl.ds(at, T)].astype(F32)
-        outs[k][...] = total.astype(BF)
-
-
-def node_kernel(mine, one, two, three, weight, upstream, act, back, term):
-    agg = (mine[...].astype(F32) + one[...].astype(F32)) + (
-        two[...].astype(F32) + three[...].astype(F32)
-    )
+def fold_kernel(parts, out):
+    total = parts[0].astype(F32)
+    for k in range(1, parts.shape[0]):
+        total += parts[k].astype(F32)
+    out[...] = total.astype(BF)
+
+
+def node_kernel(parts, weight, upstream, act, back, term):
+    agg = parts[0].astype(F32)
+    for k in range(1, parts.shape[0]):
+        agg += parts[k].astype(F32)
     agg = agg.astype(BF)
     pre = jnp.dot(agg, weight[...], preferred_element_type=F32)
     sigma = jax.nn.sigmoid(pre)
@@ -89,24 +86,24 @@
 
 
 def pack_kernel(back, got, send):
-    send[:T] = back[...]
     term = got[0].astype(F32)
     for k in range(1, 8):
         term += got[k].astype(F32)
-    send[T:] = term.astype(BF)
-
-
-def spread_kernel(mine, one, two, three, send, terms):
-    me = lax.axis_index("yh")
-    for k, part in enumerate((mine, one, two, three)):
-        h = (me + 4 - k) % 4
-        terms[h] = part[T:].astype(F32)
-        at = pl.multiple_of(h * T, T)
-        for j in range(8):
-            send[j, pl.ds(at, T)] = part[:T]
-    total = ((terms[0] + terms[1]) + (terms[2] + terms[3])).astype(BF)
+    term = term.astype(BF)
+    for h in range(4):
+        send[h, :T] = back[...]
+        send[h, T:] = term
+
+
+def spread_kernel(got, send):
+    term = got[0, T:].astype(F32)
+    for k in range(1, 4):
+        term += got[k, T:].astype(F32)
+    term = term.astype(BF)
     for j in range(8):
-        send[j, 4 * T :] = total
+        for h in range(4):
+            send[j, h * T : (h + 1) * T] = got[h, :T]
+        send[j, 4 * T :] = term
 
 
 def backward_kernel(places, count, tiles, got, keep, send, term, acc):
@@ -150,10 +147,6 @@
         term[k * 32 : k * 32 + 32] = got[k, T:].astype(F32)
 
 
-def shifted(value, by):
-    return lax.ppermute(value, "yh", [(i, (i + by) % 4) for i in range(4)])
-
-
 def per_device(features, weight, tile_values, tile_places, tile_count, upstream):
     own_rows = features[0]
     tiles = tile_values[0, 0]
@@ -167,19 +160,16 @@
         places, tile_count, tiles, own, other, scratch=[pltpu.VMEM((32, T, 256), F32)],
     )
     parts = lax.all_to_all(partial, ("x", "yl"), 0, 0)
-    parts = call(fold_kernel, (shape((T, 256)),) * 4, [VM], parts)
-    parts = [parts[0]] + [shifted(parts[k], k) for k in (1, 2, 3)]
+    parts = call(fold_kernel, shape((4 * T, 256)), [VM], parts)
+    parts = lax.all_to_all(parts.reshape(4, T, 256), "yh", 0, 0)
     act, back, term = call(
-        node_kernel, (shape((T, 256)), shape((T, 256)), shape((8, 32, 256))), [VM] * 6,
-        *parts, weight, upstream[0],
+        node_kernel, (shape((T, 256)), shape((T, 256)), shape((8, 32, 256))), [VM] * 3,
+        parts, weight, upstream[0],
     )
     term = lax.all_to_all(term, "z", 0, 0)
-    send = call(pack_kernel, shape((T + 32, 256)), [VM, VM], back, term)
-    sends = [send] + [shifted(send, k) for k in (1, 2, 3)]
-    send = call(
-        spread_kernel, shape((8, 4 * T + 32, 256)), [VM] * 4, *sends,
-        scratch=[pltpu.VMEM((4, 32, 256), F32)],
-    )
+    send = call(pack_kernel, shape((4, T + 32, 256)), [VM, VM], back, term)
+    got = lax.all_to_all(send, "yh", 0, 0)
+    send = call(spread_kernel, shape((8, 4 * T + 32, 256)), [VM], got)
     got = lax.all_to_all(send, ("x", "yl"), 0, 0)
     keep, send, term = call(
         backward_kernel, (shape((8, T, 256)), shape((8 * T + 64, 256)), shape((32, 256), F32)),

time: 181 us -> 173 us (0.956)
  blocking collectives: 118 us -> 149 us
  starting transfers between devices: 41.3 us -> 12.3 us
  waiting for transfers between devices: 11.8 us -> 2.43 us
    ppermute x6 -> x0, starting transfers between devices: 29.2 us -> none  [shifted(): return lax.ppermute(value, 'yh', [(i, (i + by) % 4) for i in range(4)])]
    all_to_all x0 -> x2, blocking collectives: none -> 27.1 us  [the longest x1 14.7 us: per_device(): parts = lax.all_to_all(parts.reshape(4, T, 256), 'yh', 0, 0)]
    ppermute x6 -> x0, waiting for transfers between devices: 9.4 us -> none  [shifted(): return lax.ppermute(value, 'yh', [(i, (i + by) % 4) for i in range(4)])]
    all_to_all x1, blocking collectives: 10.3 us -> 12.8 us  [per_device(): term = lax.all_to_all(term, 'z', 0, 0)]
    all_to_all x1, blocking collectives: 22.2 us -> 24.6 us  [per_device(): got = lax.all_to_all(send, 'z', 0, 0)]
  transfers between devices with their start and end apart: 8 -> 2, of which waited for: 6 -> 2; matrix products, arithmetic and copies ran while one was open for 0% -> 0% of each run, Pallas kernels for 0% -> 0%
where the time goes in v5:
time: 173 us; the launch traced here: 172 us
  blocking collectives  149 us (86%)
  starting transfers between devices  12.3 us (7%)
  Pallas kernels  5.55 us (3%)
  waiting for transfers between devices  2.43 us (1%)
    all_to_all x1, blocking collectives, per_device(): parts = lax.all_to_all(partial, ('x', 'yl'), 0, 0)  31.7 us
    all_to_all x1, blocking collectives, per_device(): own = lax.all_to_all(jnp.broadcast_to(own_rows, (8, T, 256)), 'z', 0, 0)  26.8 us
    all_to_all x1, blocking collectives, per_device(): got = lax.all_to_all(send, ('x', 'yl'), 0, 0)  26.2 us
    all_to_all x1, blocking collectives, per_device(): got = lax.all_to_all(send, 'z', 0, 0)  24.6 us
    all_to_all x1, blocking collectives, per_device(): parts = lax.all_to_all(parts.reshape(4, T, 256), 'yh', 0, 0)  14.7 us
    all_to_all x1, blocking collectives, per_device(): term = lax.all_to_all(term, 'z', 0, 0)  12.8 us
    all_to_all x1, blocking collectives, per_device(): got = lax.all_to_all(send, 'yh', 0, 0)  12.3 us
    ppermute x1, starting transfers between devices, per_device(): got = lax.ppermute(send, 'c', swap)  8.09 us
  transfers between devices with their start and end apart: 2, of which 2 were waited for; matrix products, arithmetic and copies ran while one was open for 0% of the time, Pallas kernels for 0%

profile of v5, /device:TPU:1, one launch (start us, length us, event | category | flops | bytes accessed | tf_op | source)
XLA Modules:
  0.0 172.4 jit_solution(8527669672535595550)
XLA Ops:
  0.6 0.0 copy-start
  0.6 1.0 broadcast_in_dim.9
  1.6 26.8 %all_to_all.35.own = bf16[8,128,256]{2,1,0:T(8,128)(2,1)S(1)} all-to-all(bf16[8,128,256]{2,1,0:T(8,128)(2,1)S(1)} %broadcast_in_dim.9), channel_id=1, replica_groups=mesh['x'=4,'yh'=4,'yl'=2,'z'=8,'c'=2] {'z'}, dimensions={0} | all-to-all | bytes 1048576 | tf_op jit(solution)/shard_map/all_to_all | solution.py:156
  28.4 4.2 %collective-permute-start = (bf16[8,128,256]{2,1,0:T(8,128)(2,1)S(1)}, bf16[8,128,256]{2,1,0:T(8,128)(2,1)S(1)}, u32[]{:S(2)}, u32[]{:S(2)}) collective-permute-start(bf16[8,128,256]{2,1,0:T(8,128)(2,1)S(1)} %all_to_all.35.own), channel_id=1, source_target_pairs={{0,1},{1,0},{2,3},{3,2},{4,5},{5,4},{6,7},{7,6},{8,9},{9,8},{10,11... | collective-permute-start | bytes 1572872 | tf_op jit(solution)/shard_map/ppermute | solution.py:157
  33.3 0.9 collective-permute-done.other
  34.2 0.0 copy-done
  34.2 0.0 copy-start.3
  34.2 0.7 copy-done.3
  34.8 1.8 %shard_map.85 = bf16[8,512,256]{2,1,0:T(8,128)(2,1)S(1)} custom-call(s32[2,48]{1,0:T(2,128)S(1)} %bitcast.11, s32[1,1]{1,0:T(1,128)S(6)} %copy.9.count, bf16[48,128,128]{2,1,0:T(8,128)(2,1)S(1)} %bitcast.7, bf16[8,128,256]{2,1,0:T(8,128)(2,1)S(1)} %all_to_all.35.own, bf16[8,128,256]{2,1,0:T(8,128)(2,1)S(1)} %collective-permute-done.other), custom_call_target="tpu_custom_call" | custom-call | tf_op jit(solution)/shard_map/pallas_call | solution.py:17
  36.6 31.7 %all_to_all.36.parts = bf16[8,512,256]{2,1,0:T(8,128)(2,1)S(1)} all-to-all(bf16[8,512,256]{2,1,0:T(8,128)(2,1)S(1)} %shard_map.85), channel_id=1, replica_groups=mesh['x'=4,'yh'=4,'yl'=2,'z'=8,'c'=2] {'x','yl'}, dimensions={0} | all-to-all | bytes 4194304 | tf_op jit(solution)/shard_map/all_to_all | solution.py:162
  68.3 0.0 copy-start.1
  68.3 0.0 copy-start.2
  68.3 0.3 shard_map.86
  68.5 14.7 %all_to_all.37.parts = bf16[4,128,256]{2,1,0:T(8,128)(2,1)S(1)} all-to-all(bf16[4,128,256]{2,1,0:T(8,128)(2,1)S(1)} %bitcast.9), channel_id=1, replica_groups=mesh['x'=4,'yh'=4,'yl'=2,'z'=8,'c'=2] {'yh'}, dimensions={0} | all-to-all | bytes 524288 | tf_op jit(solution)/shard_map/all_to_all | solution.py:164
  83.3 0.0 copy-done.1
  83.3 0.0 copy-done.2
  83.3 0.8 shard_map.87
  84.1 12.8 %all_to_all.38.got = bf16[8,32,256]{2,1,0:T(8,128)(2,1)S(1)} all-to-all(bf16[8,32,256]{2,1,0:T(8,128)(2,1)S(1)} %get-tuple-element.13), channel_id=1, replica_groups=mesh['x'=4,'yh'=4,'yl'=2,'z'=8,'c'=2] {'z'}, dimensions={0} | all-to-all | bytes 262144 | tf_op jit(solution)/shard_map/all_to_all | solution.py:169
  96.9 12.3 %all_to_all.39.got = bf16[4,160,256]{2,1,0:T(8,128)(2,1)S(1)} all-to-all(bf16[4,160,256]{2,1,0:T(8,128)(2,1)S(1)} %shard_map.88), channel_id=1, replica_groups=mesh['x'=4,'yh'=4,'yl'=2,'z'=8,'c'=2] {'yh'}, dimensions={0} | all-to-all | bytes 655360 | tf_op jit(solution)/shard_map/all_to_all | solution.py:171
  109.2 0.1 shard_map.89
  109.4 0.0 copy-start.4
  109.4 26.2 %all_to_all.40.got = bf16[8,544,256]{2,1,0:T(8,128)(2,1)S(1)} all-to-all(bf16[8,544,256]{2,1,0:T(8,128)(2,1)S(1)} %shard_map.89), channel_id=1, replica_groups=mesh['x'=4,'yh'=4,'yl'=2,'z'=8,'c'=2] {'x','yl'}, dimensions={0} | all-to-all | bytes 4456448 | tf_op jit(solution)/shard_map/all_to_all | solution.py:173
  135.6 0.0 copy-done.4
  135.6 1.6 shard_map.90
  137.2 8.1 %collective-permute-start.1 = (bf16[1088,256]{1,0:T(8,128)(2,1)S(1)}, bf16[1088,256]{1,0:T(8,128)(2,1)S(1)}, u32[]{:S(2)}, u32[]{:S(2)}) collective-permute-start(bf16[1088,256]{1,0:T(8,128)(2,1)S(1)} %get-tuple-element.15), channel_id=1, source_target_pairs={{0,1},{1,0},{2,3},{3,2},{4,5},{5,4},{6,7},{7,6},{8,9},{9,8},{10,11... | collective-permute-start | bytes 1671176 | tf_op jit(solution)/shard_map/ppermute | solution.py:179
  145.3 1.6 collective-permute-done.1.got
  146.8 0.1 shard_map.91
  147.0 24.6 %all_to_all.41.got = bf16[8,160,256]{2,1,0:T(8,128)(2,1)S(1)} all-to-all(bf16[8,160,256]{2,1,0:T(8,128)(2,1)S(1)} %shard_map.91), channel_id=1, replica_groups=mesh['x'=4,'yh'=4,'yl'=2,'z'=8,'c'=2] {'z'}, dimensions={0} | all-to-all | bytes 1310720 | tf_op jit(solution)/shard_map/all_to_all | solution.py:181
  171.6 0.8 shard_map.92
  (1 shorter events, 0.0 us)
Async XLA Ops:
  0.6 33.5 %copy-start = (bf16[1,1,48,128,128]{4,3,2,1,0:T(8,128)(2,1)S(1)}, bf16[1,1,48,128,128]{4,3,2,1,0:T(8,128)(2,1)}, u32[]{:S(2)}) copy-start(bf16[1,1,48,128,128]{4,3,2,1,0:T(8,128)(2,1)} %param.8) | copy-start | bytes 4718596
  28.4 5.8 %collective-permute-start = (bf16[8,128,256]{2,1,0:T(8,128)(2,1)S(1)}, bf16[8,128,256]{2,1,0:T(8,128)(2,1)S(1)}, u32[]{:S(2)}, u32[]{:S(2)}) collective-permute-start(bf16[8,128,256]{2,1,0:T(8,128)(2,1)S(1)} %all_to_all.35.own), channel_id=1, source_target_pairs={{0,1},{1,0},{2,3},{3,2},{4,5},{5,4},{6,7},{7,6},{8,9},{9,8},{10,11... | collective-permute-start | bytes 1572872 | tf_op jit(solution)/shard_map/ppermute | solution.py:157
  34.2 0.7 copy-start.3
  68.3 15.0 %copy-start.1 = (bf16[256,256]{1,0:T(8,128)(2,1)S(1)}, bf16[256,256]{1,0:T(8,128)(2,1)}, u32[]{:S(2)}) copy-start(bf16[256,256]{1,0:T(8,128)(2,1)} %weight.1) | copy-start | bytes 393220
  68.3 15.0 %copy-start.2 = (bf16[1,128,256]{2,1,0:T(8,128)(2,1)S(1)}, bf16[1,128,256]{2,1,0:T(8,128)(2,1)}, u32[]{:S(2)}) copy-start(bf16[1,128,256]{2,1,0:T(8,128)(2,1)} %param.11) | copy-start | bytes 196612
  109.4 26.2 %copy-start.4 = (s32[1,1,2,48]{3,2,1,0:T(2,128)S(1)}, s32[1,1,2,48]{3,2,1,0:T(2,128)}, u32[]{:S(2)}) copy-start(s32[1,1,2,48]{3,2,1,0:T(2,128)} %param.9) | copy-start | bytes 1156
  137.2 9.7 %collective-permute-start.1 = (bf16[1088,256]{1,0:T(8,128)(2,1)S(1)}, bf16[1088,256]{1,0:T(8,128)(2,1)S(1)}, u32[]{:S(2)}, u32[]{:S(2)}) collective-permute-start(bf16[1088,256]{1,0:T(8,128)(2,1)S(1)} %get-tuple-element.15), channel_id=1, source_target_pairs={{0,1},{1,0},{2,3},{3,2},{4,5},{5,4},{6,7},{7,6},{8,9},{9,8},{10,11... | collective-permute-start | bytes 1671176 | tf_op jit(solution)/shard_map/ppermute | solution.py:179
